TPU v7x, 512 devices: a whole 4x8x8 slice. The times are simulated.
512 devices in a mesh: dp: 32 (over z, x_hi, core), seq: 16 (over y, x_lo).
Axes of the slice: x: 4 (x_hi: 2, x_lo: 2; x = x_hi * 2 + x_lo), y: 8, z: 8, core: 2. Of those that a mesh axis runs over, the one named last changes fastest.
Arguments:
- features: bfloat16 [32, 2048, 1920], P('dp', 'seq'), may hold values from -48 to 48
- segment_ids: int32 [32, 2048], P('dp'), may hold values from 0 to 7, never falling along the last dimension, each value on 1 to 512 neighbouring positions
- projections: bfloat16 [3, 1920, 1920], P(None, 'seq'), may hold values from -1 to 1
- cotangent: bfloat16 [32, 2048, 1920], P('dp', 'seq'), may hold values from -6 to 6
Outputs:
- context: bfloat16 [32, 2048, 1920], P('dp', 'seq')
- value_grad: float32 [1920, 1920], P('seq')
Inputs may be any that keep to these rules, and one draw needn't show every extreme that they name: `segment_ids`: segment numbers never fall along a sequence; every utterance number appears, each utterance has 1 to 512 frames, and one has exactly 512.
All inputs are finite; a program needn't handle non-finite values.
Results may differ from a plain program's by a relative error of at most 0.011.
Values may be sent and summed in bfloat16 or wider, within the bound.
A program may use at most 64 MiB of HBM per device.

v0:
```python
import jax
import jax.numpy as jnp
from jax import lax
from jax.sharding import PartitionSpec as P

HEAD = 120


def body(features, segment_ids, projections, cotangent):
    frames_local = features[0]
    labels = segment_ids[0]
    local_width = projections.shape[1]
    head_size = HEAD
    local_heads = local_width // head_size
    model_width = frames_local.shape[1]
    weights = projections.reshape(3 * local_width, model_width)
    upstream = lax.all_to_all(cotangent[0], "seq", split_axis=1, concat_axis=0, tiled=True)
    gathered = lax.all_gather(frames_local, "seq", axis=0, tiled=True)
    projected = jnp.einsum(
        "tf,cf->tc", gathered, weights, preferred_element_type=jnp.float32
    ).astype(jnp.bfloat16)
    total_frames = projected.shape[0]
    queries = projected[:, :local_width].reshape(total_frames, local_heads, head_size)
    key_rows = projected[:, local_width : 2 * local_width].reshape(
        total_frames, local_heads, head_size
    )
    values = projected[:, 2 * local_width :].reshape(total_frames, local_heads, head_size)
    upstream_heads = upstream.reshape(total_frames, local_heads, head_size)
    block_rows = min(512, total_frames)
    block_count = total_frames // block_rows
    score_scale = head_size ** (-0.5)

    def weights_of(block_index):
        offset = block_index * block_rows
        query_block = lax.dynamic_slice_in_dim(queries, offset, block_rows, 0)
        row_labels = lax.dynamic_slice_in_dim(labels, offset, block_rows, 0)
        scores = (
            jnp.einsum("qhe,khe->hqk", query_block, key_rows, preferred_element_type=jnp.float32)
            * score_scale
        )
        same_segment = row_labels[:, None] == labels[None, :]
        scores = jnp.where(same_segment[None], scores, -1e30)
        row_max = jnp.max(scores, axis=2, keepdims=True)
        exponent = jnp.exp(scores - row_max)
        attn_weights = (exponent / jnp.sum(exponent, axis=2, keepdims=True)).astype(jnp.bfloat16)
        return (attn_weights, offset)

    def context_of(attn_weights):
        return jnp.einsum(
            "hqk,khe->qhe", attn_weights, values, preferred_element_type=jnp.float32
        ).astype(jnp.bfloat16)

    def value_term(attn_weights, offset):
        grad_block = lax.dynamic_slice_in_dim(upstream_heads, offset, block_rows, 0)
        return jnp.einsum(
            "hqk,qhe->khe", attn_weights, grad_block, preferred_element_type=jnp.float32
        )

    empty_rows = jnp.zeros((total_frames, local_heads, head_size), jnp.float32)

    def joint_step(running, block_index):
        attn_weights, offset = weights_of(block_index)
        return (running + value_term(attn_weights, offset), context_of(attn_weights))

    value_sum, blocks = lax.scan(joint_step, empty_rows, jnp.arange(block_count))
    context = blocks.reshape(total_frames, local_width)
    returned = lax.all_to_all(context, "seq", split_axis=0, concat_axis=1, tiled=True)
    value_rows = value_sum.reshape(total_frames, local_width).astype(jnp.bfloat16)
    partial_grad = jnp.einsum("tw,td->wd", value_rows, gathered, preferred_element_type=jnp.float32)
    summed = lax.psum(partial_grad, "dp")
    value_grad = summed / lax.axis_size("dp")
    return (returned[None], value_grad)


def solution(mesh):
    in_specs = (P("dp", "seq", None), P("dp", None), P(None, "seq", None), P("dp", "seq", None))
    out_specs = (P("dp", "seq", None), P("seq", None))
    return jax.shard_map(body, mesh=mesh, in_specs=in_specs, out_specs=out_specs, check_vma=False)
```

profile of v0, /device:TPU:1, one launch (start us, length us, event | category | flops | bytes accessed | tf_op | source)
XLA Modules:
  0.0 536.6 jit_solution(14925531246365811088)
XLA Ops:
  7.9 2.0 copy.15
  9.9 8.7 %all-to-all-start = ((bf16[128,16,120]{0,2,1:T(8,128)(2,1)}), bf16[128,16,120]{0,2,1:T(8,128)(2,1)S(1)}, u32[]{:S(2)}, u32[]{:S(2)}) async-start(bf16[128,16,120]{0,2,1:T(8,128)(2,1)} %bitcast), calls=%async_computation | async-start | bytes 983040 | tf_op jit(solution)/shard_map/all_to_all | solution.py:17
  18.6 14.4 %all-to-all-done = bf16[128,16,120]{0,2,1:T(8,128)(2,1)S(1)} async-done(((bf16[128,16,120]{0,2,1:T(8,128)(2,1)}), bf16[128,16,120]{0,2,1:T(8,128)(2,1)S(1)}, u32[]{:S(2)}, u32[]{:S(2)}) %all-to-all-start) | async-done | bytes 491552 | tf_op jit(solution)/shard_map/all_to_all | solution.py:17
  33.1 1.0 reshape.71
  34.1 158.1 %all-gather.3.cloned.1.call-done = bf16[1,2048,1920]{2,1,0:T(8,128)(2,1)} async-done(((bf16[1,128,1920]{2,1,0:T(8,128)(2,1)}), bf16[1,2048,1920]{2,1,0:T(8,128)(2,1)}) %all-gather.3.cloned.1.call-update) | async-done | bytes 7864336 | tf_op jit(solution)/shard_map/all_gather | solution.py:18
  192.2 6.5 %fusion.16 = bf16[2048,360]{0,1:T(8,128)(2,1)S(1)} fusion(bf16[360,1920]{1,0:T(8,128)(2,1)S(1)} %bitcast.84, bf16[1,2048,1920]{2,1,0:T(8,128)(2,1)} %all-gather.3.cloned.1.call-done), kind=kOutput, calls=%fused_computation.21 | convolution fusion | flops 2831892480 | bytes 10721280 | tf_op jit(solution)/shard_map/tf,cf->tc/dot_general | solution.py:19
  198.7 1.2 slice_bitcast_fusion
  199.9 36.9 %while.13 = (s32[]{:T(128)}, f32[2048,1,120]{0,2,1:T(8,128)}, bf16[4,512,1,120]{1,3,2,0:T(8,128)(2,1)}, s32[4]{0:T(128)S(1)}, bf16[2048,1,120]{0,2,1:T(8,128)(2,...) while((s32[]{:T(128)}, f32[2048,1,120]{0,2,1:T(8,128)}, ...), condition=%wide.region_3.4_spmd.clone, body=%wide.region_0.3_spmd.clone.sunk | while | flops 764963840 | bytes 24183536 | solution.py:65
  201.3 2.1 fusion.37
  204.0 0.8 divide_convert_fusion.2
  204.8 2.5 fusion.39
  207.3 1.5 fusion.40
  210.2 2.1 fusion.37
  213.0 0.8 divide_convert_fusion.2
  213.8 2.9 fusion.39
  216.6 1.5 fusion.40
  219.5 2.1 fusion.37
  222.3 0.8 divide_convert_fusion.2
  223.1 2.9 fusion.39
  226.0 1.5 fusion.40
  228.8 2.1 fusion.37
  231.6 0.8 divide_convert_fusion.2
  232.4 2.9 fusion.39
  235.3 1.5 fusion.40
  236.7 1.4 copy.17
  238.3 0.9 copy.18
  239.2 5.3 all-to-all-start.1
  244.6 5.5 %fusion.12 = f32[120,1920]{1,0:T(8,128)} fusion(bf16[1,2048,1920]{2,1,0:T(8,128)(2,1)} %all-gather.3.cloned.1.call-done, f32[2048,1,120]{0,2,1:T(8,128)S(1)} %copy-done.1), kind=kOutput, calls=%fused_computation.17 | convolution fusion | flops 943964160 | bytes 9768960 | tf_op jit(solution)/shard_map/tw,td->wd/dot_general | solution.py:69
  250.1 9.5 %all-to-all-done.1 = bf16[16,128,120]{1,2,0:T(8,128)(2,1)S(1)} async-done(((bf16[16,128,120]{1,2,0:T(8,128)(2,1)}), bf16[16,128,120]{1,2,0:T(8,128)(2,1)S(1)}, u32[]{:S(2)}, u32[]{:S(2)}) %all-to-all-start.1) | async-done | bytes 491552 | tf_op jit(solution)/shard_map/all_to_all | solution.py:67
  259.6 1.0 copy.19
  260.6 267.0 %all-reduce.2.cloned.1.call-done = f32[120,1920]{1,0:T(8,128)} async-done(((f32[120,1920]{1,0:T(8,128)}), f32[120,1920]{1,0:T(8,128)}) %all-reduce.2.cloned.1.call-update) | async-done | bytes 921616 | tf_op jit(solution)/shard_map/psum | solution.py:70
  527.6 2.2 broadcast_multiply_fusion
  (35 shorter events, 6.8 us)
Async XLA Ops:
  7.2 185.0 %copy-start = (bf16[3,120,1920]{2,1,0:T(8,128)(2,1)S(1)}, bf16[3,120,1920]{2,1,0:T(8,128)(2,1)}, u32[]{:S(2)}) copy-start(bf16[3,120,1920]{2,1,0:T(8,128)(2,1)} %param.8) | copy-start | bytes 4147204
  7.2 185.0 %all-gather.3.cloned.1.call-start = ((), (), s32[]{:S(2)}) async-start(), calls=%async_computation.3 | async-start | bytes 8355840 | tf_op jit(solution)/shard_map/all_gather | solution.py:18
  9.9 23.1 %all-to-all-start = ((bf16[128,16,120]{0,2,1:T(8,128)(2,1)}), bf16[128,16,120]{0,2,1:T(8,128)(2,1)S(1)}, u32[]{:S(2)}, u32[]{:S(2)}) async-start(bf16[128,16,120]{0,2,1:T(8,128)(2,1)} %bitcast), calls=%async_computation | async-start | bytes 983040 | tf_op jit(solution)/shard_map/all_to_all | solution.py:17
  192.2 7.7 %copy-start.3 = (s32[1,2048]{1,0:T(1,128)S(1)}, s32[1,2048]{1,0:T(1,128)}, u32[]{:S(2)}) copy-start(s32[1,2048]{1,0:T(1,128)} %param.7) | copy-start | bytes 24580
  204.8 2.5 copy-start.2
  213.8 2.9 copy-start.2
  223.1 2.9 copy-start.2
  232.4 2.9 copy-start.2
  236.7 7.9 %copy-start.1 = (f32[2048,1,120]{0,2,1:T(8,128)S(1)}, f32[2048,1,120]{0,2,1:T(8,128)}, u32[]{:S(2)}) copy-start(f32[2048,1,120]{0,2,1:T(8,128)} %get-tuple-element.56) | copy-start | bytes 2949124
  239.2 20.3 %all-to-all-start.1 = ((bf16[16,128,120]{1,2,0:T(8,128)(2,1)}), bf16[16,128,120]{1,2,0:T(8,128)(2,1)S(1)}, u32[]{:S(2)}, u32[]{:S(2)}) async-start(bf16[16,128,120]{1,2,0:T(8,128)(2,1)} %copy.18), calls=%async_computation.1 | async-start | bytes 983040 | tf_op jit(solution)/shard_map/all_to_all | solution.py:67
  244.6 283.0 %all-reduce.2.cloned.1.call-start = ((), (), s32[]{:S(2)}) async-start(), calls=%async_computation.2 | async-start | bytes 1843200 | tf_op jit(solution)/shard_map/psum | solution.py:70
Sparse Core Ops, SparseCore 0:
  10.1 182.0 all-gather.2
  250.2 277.2 all-reduce.1
where the time goes:
time: 537 us
  waiting for transfers between devices  450 us (84%)
  matrix products  37.2 us (7%)
  starting transfers between devices  14.1 us (3%)
  between operations  14.1 us (3%)
  local copies, waits for them, and re-layouts  10.7 us (2%)
  other arithmetic  8.07 us (2%)
    psum x1, waiting for transfers between devices, body(): summed = lax.psum(partial_grad, 'dp')  267 us
    all_gather x1, waiting for transfers between devices, body(): gathered = lax.all_gather(frames_local, 'seq', axis=0, tiled=True)  158 us
    all_to_all x1, waiting for transfers between devices, body(): lax.all_to_all(cotangent[0], 'seq', split_axis=1, concat_axis=0, tiled=True)  14.4 us
    dot_general x4, matrix products, value_term(): jnp.einsum('hqk,qhe->khe', attn_weights, grad_block, preferred_element_ty...  11.1 us
  transfers between devices with their start and end apart: 4, of which 4 were waited for; matrix products, arithmetic and copies ran while one was open for 2% of the time, Pallas kernels for 0%

commit v1 on v0

v1 whole, which is shorter than its diff:
```python
import functools

import jax
import jax.numpy as jnp
from jax import lax
from jax.experimental import pallas as pl
from jax.experimental.pallas import tpu as pltpu
from jax.sharding import PartitionSpec as P

HEAD = 120
PAD = 128
ROWS = 128
HALF = 64
WINDOW = 10
LOG2E = 1.4426950408889634
MESH = pl.DeviceIdType.MESH
NT = (((1,), (1,)), ((), ()))
NN = (((1,), (0,)), ((), ()))
TN = (((0,), (0,)), ((), ()))
F32 = jnp.float32
BF16 = jnp.bfloat16


def kernel(
    nz, feat, w, cot, seg, ctx_out, grad_out,
    G, WA, CT, DO, QKV, QS, SEGC, VRT, CX, CR, AB, AS, PB, RA, PA, RB, PC, RC, PD, RE,
    ring_s, ring_r, loc, w_s, w_r, wf_s, wf_r, qs_s, qs_r, do_s, do_r, cx_s, cx_r,
    vr_s, vr_r, a_s, a_r, b_s, b_r, c_s, c_r, d_s, d_r, e_s, e_r,
):
    ny = G.shape[0]
    ns = 2 * ny
    width = feat.shape[2]
    dp, sq = lax.axis_index("dp"), lax.axis_index("seq")
    core = lax.rem(dp, 2)
    xhi = lax.rem(lax.div(dp, 2), 2)
    z = lax.div(dp, 4)
    y = lax.div(sq, 2)
    xlo = lax.rem(sq, 2)
    peer_x = sq + 1 - 2 * xlo
    peer_core = dp + 1 - 2 * core
    peer_xhi = dp + 2 - 4 * xhi

    def remote(src, dst, ssem, rsem, dev):
        return pltpu.make_async_remote_copy(
            src_ref=src, dst_ref=dst, send_sem=ssem, recv_sem=rsem, device_id=dev, device_id_type=MESH
        )

    barrier = pltpu.get_barrier_semaphore()

    def hello(dev):
        pl.semaphore_signal(barrier, inc=1, device_id=dev, device_id_type=MESH)

    def hello_seq(d, carry):
        hello((dp, lax.rem(sq + d, ns)))
        return carry

    lax.fori_loop(1, ns, hello_seq, 0)
    hello((peer_core, sq))
    hello((peer_xhi, sq))
    hello((peer_xhi, peer_x))

    def z_dev(d):
        return lax.rem(z + d, nz) * 4 + lax.rem(dp, 4)

    def hello_z(d, carry):
        hello((z_dev(d), sq))
        return carry

    lax.fori_loop(1, nz, hello_z, 0)
    pl.semaphore_wait(barrier, ns - 1 + 3 + nz - 1)

    last = ny - 1

    def ring(dirn, k, at):
        hops = k // 2
        if dirn == 0:
            shard, half, to = lax.rem(at + ny - hops, ny), k % 2, lax.rem(sq + 2, ns)
        else:
            shard, half, to = lax.rem(at + hops, ny), 1 - k % 2, lax.rem(sq + ns - 2, ns)
        src = feat.at[half] if k < 2 else G.at[shard, half]
        return remote(src, G.at[shard, half], ring_s.at[dirn, k], ring_r.at[dirn, k], (dp, to))

    def ring_send(dirn, k):
        return ring(dirn, k, y)

    def ring_recv(dirn, k):
        return ring(dirn, k, lax.rem(y + ny - 1, ny) if dirn == 0 else lax.rem(y + 1, ny))

    for k in range(2):
        for dirn in range(2):
            ring_send(dirn, k).start()
    w_send = remote(w.at[:, core], WA.at[1, :, core], w_s, w_r, (dp, peer_x))
    w_send.start()
    own_feat = pltpu.make_async_copy(feat, G.at[y], loc.at[0])
    own_feat.start()
    own_w = pltpu.make_async_copy(w, WA.at[0], loc.at[1])
    own_w.start()

    for h in range(ns):
        CT[h] = jnp.zeros((ROWS, PAD), BF16)
        CT[h, :, 0:HEAD] = cot[:, h * HEAD : (h + 1) * HEAD]
    DO[sq] = CT[sq]

    def label_col(b, carry):
        row = seg[pl.ds(b, 1), :].astype(F32)
        SEGC[b] = jnp.broadcast_to(row, (ROWS, ROWS)).T
        return carry

    lax.fori_loop(0, ns, label_col, 0)
    VRT[...] = jnp.zeros_like(VRT)

    own_feat.wait()
    own_w.wait()

    def project(shard):
        x = G[shard].reshape(ROWS, width)
        wall = WA[...].reshape(6 * PAD, width)
        r = lax.dot_general(x, wall, NT, preferred_element_type=F32).astype(BF16)
        for p in range(3):
            QKV[2 * shard + xlo, p] = r[:, p * PAD : (p + 1) * PAD]
            QS[shard, p] = r[:, (3 + p) * PAD : (4 + p) * PAD]
        qs_copy(shard).start()

    def qs_copy(shard):
        return remote(
            QS.at[shard], QKV.at[2 * shard + xlo], qs_s.at[shard], qs_r.at[shard], (dp, peer_x)
        )

    def at_y(d):
        return lax.rem(y + d + ny, ny)

    def arrive(k):
        for dirn in range(2):
            ring_recv(dirn, k).wait_recv()
            if k + 2 <= last - 1:
                ring_send(dirn, k + 2).start()

    def do_copy(d):
        to = lax.rem(sq + d, ns)
        return remote(CT.at[to], DO.at[sq], do_s.at[to], do_r.at[sq], (dp, to))

    def do_start(t, carry):
        d = lax.rem(ny + t, ns)

        @pl.when(d != 0)
        def _():
            do_copy(d).start()

        return carry

    arrive(0)
    arrive(1)
    w_send.wait_recv()
    w_fwd = remote(WA.at[1, :, core], WA.at[1, :, core], wf_s, wf_r, (peer_core, sq))
    w_fwd.start()
    arrive(2)
    other = 1 - core
    remote(WA.at[1, :, other], WA.at[1, :, other], wf_s, wf_r, (peer_core, sq)).wait_recv()
    project(y)
    arrive(3)
    project(at_y(1))
    project(at_y(-1))
    arrive(4)
    lax.fori_loop(0, ns, do_start, 0)
    project(at_y(2))
    project(at_y(-2))
    arrive(5)
    project(at_y(3))
    project(at_y(-3))
    arrive(6)
    project(at_y(4))

    def qs_wait(t, carry):
        qs_copy(t).wait_send()
        b = 2 * t + (1 - xlo)
        remote(QS.at[t], QKV.at[b], qs_s.at[t], qs_r.at[t], (dp, peer_x)).wait_recv()
        return carry

    lax.fori_loop(0, ny, qs_wait, 0)

    scale = HEAD ** (-0.5) * LOG2E

    def do_wait(b):
        @pl.when(b != sq)
        def _():
            remote(CT.at[b], DO.at[b], do_s.at[b], do_r.at[b], (dp, b)).wait_recv()

    def cx_copy(b):
        return remote(CX.at[b], CR.at[sq], cx_s.at[b], cx_r.at[sq], (dp, b))

    def attend(t, carry):
        i = lax.rem(y + 4 + t, ny)
        s0 = jnp.clip(i - 2, 0, ny - WINDOW // 2)
        q = QKV[pl.ds(2 * i, 2), 0].reshape(2 * ROWS, PAD)
        keys = QKV[pl.ds(2 * s0, WINDOW), 1].reshape(WINDOW * ROWS, PAD)
        vals = QKV[pl.ds(2 * s0, WINDOW), 2].reshape(WINDOW * ROWS, PAD)
        s = lax.dot_general(q, keys, NT, preferred_element_type=F32)
        col = SEGC[pl.ds(2 * i, 2)].reshape(2 * ROWS, PAD)
        parts = []
        for j in range(WINDOW):
            row = seg[pl.ds(2 * s0 + j, 1), :].astype(F32)
            parts.append(jnp.where(col == row, s[:, j * PAD : (j + 1) * PAD], -1e30))
        top = functools.reduce(jnp.maximum, parts)
        top = jnp.max(top, axis=1, keepdims=True)
        es = [jnp.exp2((part - top) * scale) for part in parts]
        total = jnp.sum(functools.reduce(jnp.add, es), axis=1, keepdims=True)
        inv = 1.0 / total
        e = jnp.concatenate([part.astype(BF16) for part in es], axis=1)
        ctx = lax.dot_general(e, vals, NN, preferred_element_type=F32) * inv
        CX[pl.ds(2 * i, 2)] = ctx.astype(BF16).reshape(2, ROWS, PAD)
        for c in range(2):
            b = 2 * i + c

            @pl.when(b != sq)
            def _(b=b):
                cx_copy(b).start()

            do_wait(b)
        up = DO[pl.ds(2 * i, 2)].reshape(2 * ROWS, PAD).astype(F32) * inv
        vr = lax.dot_general(up.astype(BF16), e, TN, preferred_element_type=F32)
        for j in range(WINDOW // 2):
            VRT[s0 + j] += vr[:, j * 2 * PAD : (j + 1) * 2 * PAD]
        return carry

    lax.fori_loop(0, ny, attend, 0)
    CR[sq] = CX[sq]

    for t in range(ny):
        v = VRT[t].astype(BF16)
        left, right = v[:, :PAD], v[:, PAD:]
        AB[xlo, t] = jnp.where(xlo == 0, left, right)
        AS[t] = jnp.where(xlo == 0, right, left)
    vr_send = remote(AS, AB.at[xlo], vr_s, vr_r, (dp, peer_x))
    vr_send.start()
    remote(AS, AB.at[1 - xlo], vr_s, vr_r, (dp, peer_x)).wait_recv()

    lhs = jnp.concatenate(
        [jnp.concatenate([AB[h, t] for t in range(ny)], axis=1) for h in range(2)], axis=0
    )
    group = 512
    for g in range(4):
        lo, hi = g * group, min((g + 1) * group, width)
        rhs = G[:, :, :, lo:hi].reshape(ny * ROWS, hi - lo)
        part = lax.dot_general(lhs, rhs, NN, preferred_element_type=F32).astype(BF16)
        if hi - lo < group:
            part = jnp.concatenate([part, jnp.zeros((2 * PAD, group - (hi - lo)), BF16)], axis=1)
        for h in range(2):
            PB[g % 2, h, g // 2] = part[h * PAD : (h + 1) * PAD].reshape(8, 16, group)

    a_send = remote(PB.at[other], RA, a_s, a_r, (peer_core, sq))
    a_send.start()
    a_send.wait_recv()
    for h in range(2):
        for g in range(2):
            PA[h, g] = (PB[core, h, g].astype(F32) + RA[h, g].astype(F32)).astype(BF16)

    def b_copy(n):
        hi, lo = (xhi, 1 - xlo) if n == 0 else (1 - xhi, xlo) if n == 1 else (1 - xhi, 1 - xlo)
        dev = (dp if n == 0 else peer_xhi, sq if n == 1 else peer_x)
        return remote(PA.at[lo, hi], RB.at[n], b_s.at[n], b_r.at[n], dev)

    for n in (2, 1, 0):
        b_copy(n).start()
    for n in range(3):
        b_copy(n).wait_recv()
    total = PA[xlo, xhi].astype(F32)
    for n in range(3):
        total += RB[n].astype(F32)
    PC[...] = total.astype(BF16)

    rows = 8 // nz

    def c_copy(d):
        to = lax.rem(z + d, nz)
        return remote(
            PC.at[pl.ds(to * rows, rows)], RC.at[d], c_s.at[d], c_r.at[d], (z_dev(d), sq)
        )

    for d in range(1, nz):
        c_copy(d).start()
    total = PC[pl.ds(z * rows, rows)].astype(F32)
    for d in range(1, nz):
        c_copy(d).wait_recv()
        total += RC[d].astype(F32)
    PD[...] = total.astype(BF16)
    mine = pl.ds(z * rows, rows)
    RE[xhi, core, mine] = total.astype(BF16)

    def d_copy(d):
        return remote(PD, RE.at[xhi, core, mine], d_s.at[d], d_r.at[d], (z_dev(d), sq))

    for d in range(1, nz):
        d_copy(d).start()
    for d in range(1, nz):
        frm = lax.rem(z + nz - d, nz)
        remote(
            PD, RE.at[xhi, core, pl.ds(frm * rows, rows)], d_s.at[d], d_r.at[d], (z_dev(d), sq)
        ).wait_recv()

    def e_copy(n):
        if n == 0:
            ref, dev = RE.at[xhi, core], (peer_xhi, sq)
        elif n == 1:
            ref, dev = RE.at[xhi, core], (peer_core, sq)
        else:
            ref, dev = RE.at[1 - xhi, core], (peer_core, sq)
        return remote(ref, ref, e_s.at[n], e_r.at[n], dev)

    def e_recv(n):
        if n == 0:
            ref, dev = RE.at[1 - xhi, core], (peer_xhi, sq)
        elif n == 1:
            ref, dev = RE.at[xhi, other], (peer_core, sq)
        else:
            ref, dev = RE.at[1 - xhi, other], (peer_core, sq)
        remote(ref, ref, e_s.at[n], e_r.at[n], dev).wait_recv()

    e_copy(0).start()
    e_copy(1).start()

    def cx_wait(b, carry):
        @pl.when(b != sq)
        def _():
            remote(CX.at[b], CR.at[b], cx_s.at[b], cx_r.at[b], (dp, b)).wait_recv()
            cx_copy(b).wait_send()
            remote(CT.at[b], DO.at[sq], do_s.at[b], do_r.at[sq], (dp, b)).wait_send()

        return carry

    lax.fori_loop(0, ns, cx_wait, 0)
    for h in range(ns):
        ctx_out[:, h * HEAD : (h + 1) * HEAD] = CR[h, :, 0:HEAD]

    e_recv(0)
    e_copy(2).start()
    e_recv(1)
    e_recv(2)
    for g in range(4):
        lo, hi = g * group, min((g + 1) * group, width)
        block = RE[g // 2, g % 2].reshape(PAD, group)[:HEAD, : hi - lo]
        grad_out[:, lo:hi] = block.astype(F32) * (1.0 / (4 * nz))

    for k in range(last):
        for dirn in range(2):
            ring_send(dirn, k).wait_send()
    w_send.wait_send()
    w_fwd.wait_send()
    vr_send.wait_send()
    a_send.wait_send()
    for n in range(3):
        b_copy(n).wait_send()
        e_copy(n).wait_send()
    for d in range(1, nz):
        c_copy(d).wait_send()
        d_copy(d).wait_send()


def body(nz, features, segment_ids, projections, cotangent):
    ns = lax.axis_size("seq")
    ny = ns // 2
    width = features.shape[2]
    feat = features.reshape(2, HALF, width)
    w = jnp.pad(projections, ((0, 0), (0, PAD - HEAD), (0, 0))).reshape(3, 2, HALF, width)
    seg = segment_ids.reshape(ns, ROWS)
    vmem = lambda *shape: pltpu.VMEM(shape, BF16)
    dma = lambda *shape: pltpu.SemaphoreType.DMA(shape)
    rows = 8 // nz
    ctx, grad = pl.pallas_call(
        functools.partial(kernel, nz),
        out_shape=(
            jax.ShapeDtypeStruct((ROWS, width), BF16),
            jax.ShapeDtypeStruct((HEAD, width), F32),
        ),
        in_specs=[pl.BlockSpec(memory_space=pltpu.VMEM)] * 4,
        out_specs=[pl.BlockSpec(memory_space=pltpu.VMEM)] * 2,
        scratch_shapes=[
            vmem(ny, 2, HALF, width),
            vmem(2, 3, 2, HALF, width),
            vmem(ns, ROWS, PAD),
            vmem(ns, ROWS, PAD),
            vmem(ns, 3, ROWS, PAD),
            vmem(ny, 3, ROWS, PAD),
            pltpu.VMEM((ns, ROWS, ROWS), F32),
            pltpu.VMEM((ny, PAD, 2 * ROWS), F32),
            vmem(ns, ROWS, PAD),
            vmem(ns, ROWS, PAD),
            vmem(2, ny, PAD, ROWS),
            vmem(ny, PAD, ROWS),
            vmem(2, 2, 2, 8, 16, 512),
            vmem(2, 2, 8, 16, 512),
            vmem(2, 2, 8, 16, 512),
            vmem(3, 8, 16, 512),
            vmem(8, 16, 512),
            vmem(nz, rows, 16, 512),
            vmem(rows, 16, 512),
            vmem(2, 2, 8, 16, 512),
            dma(2, ny - 1), dma(2, ny - 1),
            dma(2),
            dma(), dma(), dma(), dma(),
            dma(ny), dma(ny),
            dma(ns), dma(ns),
            dma(ns), dma(ns),
            dma(), dma(), dma(), dma(),
            dma(3), dma(3),
            dma(nz), dma(nz),
            dma(nz), dma(nz),
            dma(3), dma(3),
        ],
        compiler_params=pltpu.CompilerParams(
            collective_id=0, has_side_effects=True, vmem_limit_bytes=60 * 1024 * 1024
        ),
    )(feat, w, cotangent[0], seg)
    return (ctx[None], grad)


def solution(mesh):
    in_specs = (P("dp", "seq", None), P("dp", None), P(None, "seq", None), P("dp", "seq", None))
    out_specs = (P("dp", "seq", None), P("seq", None))
    step = functools.partial(body, mesh.shape["dp"] // 4)
    return jax.shard_map(step, mesh=mesh, in_specs=in_specs, out_specs=out_specs, check_vma=False)
```

time: 537 us -> 122 us (0.23)
  waiting for transfers between devices: 450 us -> 0 us
  Pallas kernels: 0 us -> 116 us
  matrix products: 37.2 us -> 0 us
  starting transfers between devices: 14.1 us -> 0 us
  between operations: 14.1 us -> 0.65 us
  other arithmetic: 8.07 us -> 0 us
    psum x1 -> x0, waiting for transfers between devices: 267 us -> none  [body(): summed = lax.psum(partial_grad, 'dp')]
    all_gather x1 -> x0, waiting for transfers between devices: 158 us -> none  [body(): gathered = lax.all_gather(frames_local, 'seq', axis=0, tiled=True)]
    pallas_call x0 -> x1, Pallas kernels: none -> 116 us  [body(): pl.pallas_call(functools.partial(kernel, nz), out_shape=(jax.ShapeDtypeSt...]
    dot_general x14 -> x0, matrix products: 37.2 us -> none  [the longest x4 11.1 us: value_term(): jnp.einsum('hqk,qhe->khe', attn_weights, grad_block, preferred_element_ty...]
    all_to_all x2 -> x0, waiting for transfers between devices: 23.9 us -> none  [the longest x1 14.4 us: body(): lax.all_to_all(cotangent[0], 'seq', split_axis=1, concat_axis=0, tiled=True)]
    all_to_all x2 -> x0, starting transfers between devices: 14 us -> none  [the longest x1 8.67 us: body(): lax.all_to_all(cotangent[0], 'seq', split_axis=1, concat_axis=0, tiled=True)]
  transfers between devices with their start and end apart: 4 -> 0, of which waited for: 4 -> 0; matrix products, arithmetic and copies ran while one was open for 2% -> 0% of each run, Pallas kernels for 0% -> 0%
where the time goes in v1:
time: 122 us
  Pallas kernels  116 us (95%)
  local copies, waits for them, and re-layouts  5.46 us (4%)
    pallas_call x1, Pallas kernels, body(): pl.pallas_call(functools.partial(kernel, nz), out_shape=(jax.ShapeDtypeSt...  116 us
    unnamed x4, local copies, waits for them, and re-layouts  2.85 us
    pad x1, local copies, waits for them, and re-layouts, body(): jnp.pad(projections, ((0, 0), (0, PAD - HEAD), (0, 0)))  2.61 us

profile of v1, /device:TPU:1, one launch (start us, length us, event | category | flops | bytes accessed | tf_op | source)
XLA Modules:
  0.0 122.0 jit_solution(6361507331644181934)
XLA Ops:
  0.6 2.6 %pad.4 = bf16[3,128,1920]{2,1,0:T(8,128)(2,1)} pad(bf16[3,120,1920]{2,1,0:T(8,128)(2,1)} %param.6, bf16[]{:T(256)} %constant.2.clone.1), padding=0_0x0_8x0_0 | pad | bytes 2856962 | tf_op jit(solution)/shard_map/jit(_pad)/pad | solution.py:363
  3.2 115.9 %shard_map.59 = (bf16[128,1920]{1,0:T(8,128)(2,1)}, f32[120,1920]{1,0:T(8,128)}) custom-call(bf16[2,64,1920]{2,1,0:T(8,128)(2,1)} %bitcast.6, bf16[3,2,64,1920]{3,2,1,0:T(8,128)(2,1)} %bitcast.5, bf16[128,1920]{1,0:T(8,128)(2,1)} %bitcast.7, s32[16,128]{1,0:T(8,128)} %bitcast.9), custom_call_target="tpu_custom_call" | custom-call | tf_op jit(solution)/shard_map/pallas_call | solution.py:368
  119.1 0.0 copy-start
  119.1 1.9 %copy.8 = bf16[1,128,1920]{2,1,0:T(8,128)(2,1)} copy(bf16[1,128,1920]{2,1,0:T(8,128)(2,1)} %bitcast.8) | data formatting | bytes 983040
  121.1 0.0 copy-done
  121.1 0.9 copy.9
Async XLA Ops:
  119.1 1.9 %copy-start = (f32[120,1920]{1,0:T(8,128)S(1)}, f32[120,1920]{1,0:T(8,128)}, u32[]{:S(2)}) copy-start(f32[120,1920]{1,0:T(8,128)} %get-tuple-element.9) | copy-start | bytes 2764804

commit v2 on v1

v2 whole, which is shorter than its diff:
```python
import functools

import jax
import jax.numpy as jnp
from jax import lax
from jax.experimental import pallas as pl
from jax.experimental.pallas import tpu as pltpu
from jax.sharding import PartitionSpec as P

HEAD = 120
PAD = 128
ROWS = 128
HALF = 64
REACH = 2
STREAMS = 2
GROUP = 512
LOG2E = 1.4426950408889634
MESH = pl.DeviceIdType.MESH
NT = (((1,), (1,)), ((), ()))
NN = (((1,), (0,)), ((), ()))
TN = (((0,), (0,)), ((), ()))
F32 = jnp.float32
BF16 = jnp.bfloat16


def kernel(
    nz, feat, w, cot, seg, CR, RE,
    G, WR, WA, CO, CT, DO, QKV, QS, SEGC, EB, INV, VRT, CX, AB, AS, PB, RA, PA, RB, PC, RC, PD,
    ring_s, ring_r, loc, w_s, w_r, wz_s, wz_r, wc_s, wc_r, qs_s, qs_r, do_s, do_r, cx_s, cx_r,
    vr_s, vr_r, a_s, a_r, b_s, b_r, c_s, c_r, d_s, d_r, e_s, e_r,
):
    ny = G.shape[0]
    ns = 2 * ny
    width = feat.shape[2]
    dp, sq = lax.axis_index("dp"), lax.axis_index("seq")
    core = lax.rem(dp, 2)
    xhi = lax.rem(lax.div(dp, 2), 2)
    z = lax.div(dp, 4)
    zlo = lax.rem(z, 2)
    y = lax.div(sq, 2)
    xlo = lax.rem(sq, 2)
    other = 1 - core
    peer_x = sq + 1 - 2 * xlo
    peer_core = dp + 1 - 2 * core
    peer_xhi = dp + 2 - 4 * xhi
    peer_z = dp + 4 - 8 * zlo

    def remote(src, dst, ssem, rsem, dev):
        return pltpu.make_async_remote_copy(
            src_ref=src, dst_ref=dst, send_sem=ssem, recv_sem=rsem, device_id=dev, device_id_type=MESH
        )

    own_feat = pltpu.make_async_copy(feat, G.at[y], loc.at[0])
    own_w = pltpu.make_async_copy(w, WR, loc.at[1])
    own_cot = pltpu.make_async_copy(cot, CO, loc.at[2])
    own_feat.start()
    own_w.start()
    own_cot.start()

    barrier = pltpu.get_barrier_semaphore()

    def hello(dev):
        pl.semaphore_signal(barrier, inc=1, device_id=dev, device_id_type=MESH)

    def hello_seq(d, carry):
        hello((dp, lax.rem(sq + d, ns)))
        return carry

    lax.fori_loop(1, ns, hello_seq, 0)
    hello((peer_core, sq))
    hello((peer_xhi, sq))
    hello((peer_xhi, peer_x))

    def z_dev(d):
        return lax.rem(z + d, nz) * 4 + lax.rem(dp, 4)

    def hello_z(d, carry):
        hello((z_dev(d), sq))
        return carry

    lax.fori_loop(1, nz, hello_z, 0)

    own_w.wait()
    quarter = HALF // 2
    for p in range(3):
        for c in range(4):
            lo = c * quarter
            hi = min(lo + quarter, HEAD)
            WA[0, p, c // 2, c % 2, 0 : hi - lo] = WR[p, lo:hi]
            if hi - lo < quarter:
                WA[0, p, c // 2, c % 2, hi - lo :] = jnp.zeros((quarter - hi + lo, width), BF16)
    own_feat.wait()
    pl.semaphore_wait(barrier, ns - 1 + 3 + nz - 1)

    last = ny - 1

    def ring(dirn, k, at):
        hops = k // 2
        if dirn == 0:
            shard, half, to = lax.rem(at + ny - hops, ny), k % 2, lax.rem(sq + 2, ns)
        else:
            shard, half, to = lax.rem(at + hops, ny), 1 - k % 2, lax.rem(sq + ns - 2, ns)
        ref = G.at[shard, half]
        return remote(ref, ref, ring_s.at[dirn, k], ring_r.at[dirn, k], (dp, to))

    def ring_send(dirn, k):
        return ring(dirn, k, y)

    def ring_recv(dirn, k):
        return ring(dirn, k, lax.rem(y + ny - 1, ny) if dirn == 0 else lax.rem(y + 1, ny))

    for k in range(2):
        for dirn in range(2):
            ring_send(dirn, k).start()

    def w_x(p):
        return remote(
            WA.at[0, p, core, zlo], WA.at[1, p, core, zlo], w_s.at[p], w_r.at[p], (dp, peer_x)
        )

    def w_z(p, at):
        ref = WA.at[1, p, core, at]
        return remote(ref, ref, wz_s.at[p], wz_r.at[p], (peer_z, sq))

    def w_c(p, c, at, n):
        ref = WA.at[1, p, c, at]
        return remote(ref, ref, wc_s.at[n, p], wc_r.at[n, p], (peer_core, sq))

    for p in range(3):
        w_x(p).start()

    own_cot.wait()
    for h in range(ns):
        CT[h] = jnp.zeros((ROWS, PAD), BF16)
        CT[h, :, 0:HEAD] = CO[:, h * HEAD : (h + 1) * HEAD]
    DO[sq] = CT[sq]

    def label_col(b, carry):
        row = seg[pl.ds(b, 1), :].astype(F32)
        SEGC[b] = jnp.broadcast_to(row, (ROWS, ROWS)).T
        return carry

    lax.fori_loop(0, ns, label_col, 0)
    VRT[...] = jnp.zeros_like(VRT)

    def at_y(d):
        return lax.rem(y + d + ny, ny)

    def arrive(k):
        for dirn in range(2):
            ring_recv(dirn, k).wait_recv()
            if k + 2 <= last - 1:
                ring_send(dirn, k + 2).start()

    for p in range(3):
        w_x(p).wait_recv()
        w_z(p, zlo).start()
        w_c(p, core, zlo, 0).start()
    arrive(0)
    for p in range(3):
        w_z(p, 1 - zlo).wait_recv()
        w_c(p, core, 1 - zlo, 1).start()
    arrive(1)

    def qs_copy(shard):
        return remote(
            QS.at[shard], QKV.at[2 * shard + xlo], qs_s.at[shard], qs_r.at[shard], (dp, peer_x)
        )

    def project(shard):
        x = G[shard].reshape(ROWS, width)
        wall = WA[...].reshape(6 * PAD, width)
        r = lax.dot_general(x, wall, NT, preferred_element_type=F32).astype(BF16)
        for p in range(3):
            QS[shard, p] = r[:, (3 + p) * PAD : (4 + p) * PAD]
        qs_copy(shard).start()
        for p in range(3):
            QKV[2 * shard + xlo, p] = r[:, p * PAD : (p + 1) * PAD]

    def qs_wait(shard):
        b = 2 * shard + (1 - xlo)
        remote(
            QS.at[shard], QKV.at[b], qs_s.at[shard], qs_r.at[shard], (dp, peer_x)
        ).wait_recv()

    def do_copy(to):
        return remote(CT.at[to], DO.at[sq], do_s.at[to], do_r.at[sq], (dp, to))

    def do_start(cross):
        col = xlo + cross - 2 * cross * xlo
        for d in (4, 3, -3, 2, -2, 1, -1):
            do_copy(2 * at_y(d) + col).start()
        if cross:
            do_copy(2 * y + col).start()

    scale = HEAD ** (-0.5) * LOG2E

    def rows_of(p, r):
        return QKV[pl.ds(2 * r, 2), p].reshape(2 * ROWS, PAD)

    def attend(i):
        q = rows_of(0, i)
        col = SEGC[pl.ds(2 * i, 2)].reshape(2 * ROWS, PAD)
        parts = []
        for o in range(-REACH, REACH + 1):
            r = lax.rem(i + o + ny, ny)
            s = lax.dot_general(q, rows_of(1, r), NT, preferred_element_type=F32)
            for c in range(2):
                row = seg[pl.ds(2 * r + c, 1), :].astype(F32)
                parts.append(jnp.where(col == row, s[:, c * PAD : (c + 1) * PAD], -1e30))
        top = functools.reduce(jnp.maximum, parts)
        top = jnp.max(top, axis=1, keepdims=True)
        total = jnp.zeros((2 * ROWS, PAD), F32)
        ctx = jnp.zeros((2 * ROWS, PAD), F32)
        for n in range(2 * REACH + 1):
            left, right = (jnp.exp2((part - top) * scale) for part in parts[2 * n : 2 * n + 2])
            total += left + right
            e = jnp.concatenate([left.astype(BF16), right.astype(BF16)], axis=1)
            EB[i, n] = e
            r = lax.rem(i + n - REACH + ny, ny)
            ctx += lax.dot_general(e, rows_of(2, r), NN, preferred_element_type=F32)
        inv = jnp.broadcast_to(1.0 / jnp.sum(total, axis=1, keepdims=True), (2 * ROWS, PAD))
        INV[i] = inv
        CX[pl.ds(2 * i, 2)] = (ctx * inv).astype(BF16).reshape(2, ROWS, PAD)

    def attend_at(d, carry):
        attend(at_y(d))
        return carry

    arrive(2)
    for p in range(3):
        w_c(p, other, zlo, 0).wait_recv()
        w_c(p, other, 1 - zlo, 1).wait_recv()
    project(y)
    arrive(3)
    project(at_y(1))
    project(at_y(-1))
    arrive(4)
    do_start(0)
    project(at_y(2))
    project(at_y(-2))
    arrive(5)
    project(at_y(3))
    project(at_y(-3))
    for d in (0, 1, -1, 2, -2):
        qs_wait(at_y(d))
    attend(y)
    arrive(6)
    project(at_y(4))
    do_start(1)
    qs_wait(at_y(3))
    qs_wait(at_y(-3))
    qs_wait(at_y(4))
    lax.fori_loop(1, ny, attend_at, 0)

    def vr_copy(r):
        return remote(AS.at[r], AB.at[xlo, r], vr_s.at[r], vr_r.at[r], (dp, peer_x))

    def value_rows_out(r):
        v = VRT[r].astype(BF16)
        left, right = v[:, :PAD], v[:, PAD:]
        AS[r] = jnp.where(xlo == 0, right, left)
        vr_copy(r).start()
        AB[xlo, r] = jnp.where(xlo == 0, left, right)

    def do_wait(b):
        @pl.when(b != sq)
        def _():
            remote(CT.at[b], DO.at[b], do_s.at[b], do_r.at[b], (dp, b)).wait_recv()

    def value_step(t, carry):
        i = lax.rem(y + 4 + t, ny)
        do_wait(2 * i)
        do_wait(2 * i + 1)
        up = DO[pl.ds(2 * i, 2)].reshape(2 * ROWS, PAD).astype(F32) * INV[i]
        up = up.astype(BF16)
        for n in range(2 * REACH + 1):
            r = lax.rem(i + n - REACH + ny, ny)
            VRT[r] += lax.dot_general(up, EB[i, n], TN, preferred_element_type=F32)

        @pl.when(t >= 4)
        def _():
            value_rows_out(lax.rem(y + 2 + t, ny))

        return carry

    lax.fori_loop(0, ny, value_step, 0)
    for d in range(2, 6):
        value_rows_out(at_y(d))

    def cx_copy(b):
        return remote(CX.at[b], CR.at[sq], cx_s.at[b], cx_r.at[sq], (dp, b))

    def cx_start(d, carry):
        cx_copy(lax.rem(sq + d, ns)).start()
        return carry

    lax.fori_loop(1, ns, cx_start, 0)
    CR[sq] = CX[sq]

    for r in range(ny):
        remote(AS.at[r], AB.at[1 - xlo, r], vr_s.at[r], vr_r.at[r], (dp, peer_x)).wait_recv()
    lhs = jnp.concatenate(
        [jnp.concatenate([AB[h, t] for t in range(ny)], axis=1) for h in range(2)], axis=0
    )
    lanes = GROUP // STREAMS

    def a_copy(u):
        return remote(PB.at[u, other], RA.at[u], a_s.at[u], a_r.at[u], (peer_core, sq))

    for u in range(STREAMS):
        for g in range(4):
            lo = g * GROUP + u * lanes
            hi = min(lo + lanes, width)
            rhs = G[:, :, :, lo:hi].reshape(ny * ROWS, hi - lo)
            part = lax.dot_general(lhs, rhs, NN, preferred_element_type=F32).astype(BF16)
            if hi - lo < lanes:
                part = jnp.concatenate([part, jnp.zeros((2 * PAD, lanes - hi + lo), BF16)], axis=1)
            for h in range(2):
                PB[u, g % 2, h, g // 2] = part[h * PAD : (h + 1) * PAD].reshape(8, 16, lanes)
        a_copy(u).start()

    def b_copy(u, n):
        hi, lo = (xhi, 1 - xlo) if n == 0 else (1 - xhi, xlo) if n == 1 else (1 - xhi, 1 - xlo)
        dev = (dp if n == 0 else peer_xhi, sq if n == 1 else peer_x)
        return remote(PA.at[u, lo, hi], RB.at[u, n], b_s.at[u, n], b_r.at[u, n], dev)

    for u in range(STREAMS):
        a_copy(u).wait_recv()
        for h in range(2):
            for g in range(2):
                PA[u, h, g] = (PB[u, core, h, g].astype(F32) + RA[u, h, g].astype(F32)).astype(BF16)
        for n in (1, 2, 0):
            b_copy(u, n).start()

    rows = 8 // nz

    def c_copy(u, d):
        to = lax.rem(z + d, nz)
        return remote(
            PC.at[u, pl.ds(to * rows, rows)], RC.at[u, d], c_s.at[u, d], c_r.at[u, d], (z_dev(d), sq)
        )

    for u in range(STREAMS):
        total = PA[u, xlo, xhi].astype(F32)
        for n in range(3):
            b_copy(u, n).wait_recv()
            total += RB[u, n].astype(F32)
        PC[u] = total.astype(BF16)
        for d in range(1, nz):
            c_copy(u, d).start()

    def d_copy(u, d, frm):
        return remote(
            PD.at[u],
            RE.at[u, xhi, core, pl.ds(frm * rows, rows)],
            d_s.at[u, d],
            d_r.at[u, d],
            (z_dev(d), sq),
        )

    for u in range(STREAMS):
        total = PC[u, pl.ds(z * rows, rows)].astype(F32)
        for d in range(1, nz):
            c_copy(u, d).wait_recv()
            total += RC[u, d].astype(F32)
        PD[u] = total.astype(BF16)
        for d in range(1, nz):
            d_copy(u, d, z).start()
        RE[u, xhi, core, pl.ds(z * rows, rows)] = total.astype(BF16)

    def e_copy(u, n, recv=False):
        c = other if recv and n > 0 else core
        hi = 1 - xhi if (n == 2) != (recv and n == 0) else xhi
        ref = RE.at[u, hi, c]
        dev = (peer_xhi if n == 0 else peer_core, sq)
        return remote(ref, ref, e_s.at[u, n], e_r.at[u, n], dev)

    for u in range(STREAMS):
        for d in range(1, nz):
            d_copy(u, d, lax.rem(z + nz - d, nz)).wait_recv()
        e_copy(u, 0).start()
        e_copy(u, 1).start()

    def cx_wait(b, carry):
        @pl.when(b != sq)
        def _():
            remote(CX.at[b], CR.at[b], cx_s.at[b], cx_r.at[b], (dp, b)).wait_recv()
            cx_copy(b).wait_send()
            do_copy(b).wait_send()

        return carry

    lax.fori_loop(0, ns, cx_wait, 0)

    for u in range(STREAMS):
        e_copy(u, 0, True).wait_recv()
        e_copy(u, 2).start()

    for k in range(last):
        for dirn in range(2):
            ring_send(dirn, k).wait_send()
    for p in range(3):
        w_x(p).wait_send()
        w_z(p, zlo).wait_send()
        w_c(p, core, zlo, 0).wait_send()
        w_c(p, core, 1 - zlo, 1).wait_send()
    for r in range(ny):
        qs_copy(r).wait_send()
        vr_copy(r).wait_send()
    for u in range(STREAMS):
        a_copy(u).wait_send()
        for n in range(3):
            b_copy(u, n).wait_send()
        for d in range(1, nz):
            c_copy(u, d).wait_send()
            d_copy(u, d, z).wait_send()
        for n in range(1, 3):
            e_copy(u, n, True).wait_recv()
        for n in range(3):
            e_copy(u, n).wait_send()


def finish(scale, cr_in, re_in, ctx_out, grad_out, cr, re, sem):
    copies = [pltpu.make_async_copy(*pair, sem.at[n]) for n, pair in enumerate(((cr_in, cr), (re_in, re)))]
    for copy in copies:
        copy.start()
    copies[0].wait()
    for h in range(cr.shape[0]):
        ctx_out[:, h * HEAD : (h + 1) * HEAD] = cr[h, :, 0:HEAD]
    copies[1].wait()
    lanes = GROUP // STREAMS
    width = grad_out.shape[1]
    for u in range(STREAMS):
        for g in range(4):
            lo = g * GROUP + u * lanes
            hi = min(lo + lanes, width)
            block = re[u, g // 2, g % 2].reshape(PAD, lanes)[:HEAD, : hi - lo]
            grad_out[:, lo:hi] = block.astype(F32) * scale


def body(nz, features, segment_ids, projections, cotangent):
    ns = lax.axis_size("seq")
    ny = ns // 2
    width = features.shape[2]
    feat = features.reshape(2, HALF, width)
    seg = segment_ids.reshape(ns, ROWS)
    vmem = lambda *shape: pltpu.VMEM(shape, BF16)
    dma = lambda *shape: pltpu.SemaphoreType.DMA(shape)
    rows = 8 // nz
    lanes = GROUP // STREAMS
    reach = 2 * REACH + 1
    held = pl.BlockSpec(memory_space=pltpu.VMEM)
    far = pl.BlockSpec(memory_space=pltpu.HBM)
    kept = pl.BlockSpec(memory_space=pl.ANY)
    cr, re = pl.pallas_call(
        functools.partial(kernel, nz),
        out_shape=(
            jax.ShapeDtypeStruct((ns, ROWS, PAD), BF16),
            jax.ShapeDtypeStruct((STREAMS, 2, 2, 8, 16, lanes), BF16),
        ),
        in_specs=[far, far, far, held],
        out_specs=[held, held],
        scratch_shapes=[
            vmem(ny, 2, HALF, width),
            vmem(3, HEAD, width),
            vmem(2, 3, 2, 2, HALF // 2, width),
            vmem(ROWS, width),
            vmem(ns, ROWS, PAD),
            vmem(ns, ROWS, PAD),
            vmem(ns, 3, ROWS, PAD),
            vmem(ny, 3, ROWS, PAD),
            pltpu.VMEM((ns, ROWS, ROWS), F32),
            vmem(ny, reach, 2 * ROWS, 2 * ROWS),
            pltpu.VMEM((ny, 2 * ROWS, PAD), F32),
            pltpu.VMEM((ny, PAD, 2 * ROWS), F32),
            vmem(ns, ROWS, PAD),
            vmem(2, ny, PAD, ROWS),
            vmem(ny, PAD, ROWS),
            vmem(STREAMS, 2, 2, 2, 8, 16, lanes),
            vmem(STREAMS, 2, 2, 8, 16, lanes),
            vmem(STREAMS, 2, 2, 8, 16, lanes),
            vmem(STREAMS, 3, 8, 16, lanes),
            vmem(STREAMS, 8, 16, lanes),
            vmem(STREAMS, nz, rows, 16, lanes),
            vmem(STREAMS, rows, 16, lanes),
            dma(2, ny - 1), dma(2, ny - 1),
            dma(3),
            dma(3), dma(3), dma(3), dma(3), dma(2, 3), dma(2, 3),
            dma(ny), dma(ny),
            dma(ns), dma(ns),
            dma(ns), dma(ns),
            dma(ny), dma(ny),
            dma(STREAMS), dma(STREAMS),
            dma(STREAMS, 3), dma(STREAMS, 3),
            dma(STREAMS, nz), dma(STREAMS, nz),
            dma(STREAMS, nz), dma(STREAMS, nz),
            dma(STREAMS, 3), dma(STREAMS, 3),
        ],
        compiler_params=pltpu.CompilerParams(
            collective_id=0, has_side_effects=True, vmem_limit_bytes=62 * 1024 * 1024
        ),
    )(feat, projections, cotangent[0], seg)
    ctx, grad = pl.pallas_call(
        functools.partial(finish, 1.0 / (4 * nz)),
        out_shape=(
            jax.ShapeDtypeStruct((ROWS, width), BF16),
            jax.ShapeDtypeStruct((HEAD, width), F32),
        ),
        in_specs=[kept, kept],
        out_specs=[held, held],
        scratch_shapes=[
            vmem(ns, ROWS, PAD),
            vmem(STREAMS, 2, 2, 8, 16, lanes),
            dma(2),
        ],
    )(cr, re)
    return (ctx[None], grad)


def solution(mesh):
    in_specs = (P("dp", "seq", None), P("dp", None), P(None, "seq", None), P("dp", "seq", None))
    out_specs = (P("dp", "seq", None), P("seq", None))
    step = functools.partial(body, mesh.shape["dp"] // 4)
    return jax.shard_map(step, mesh=mesh, in_specs=in_specs, out_specs=out_specs, check_vma=False)
```

time: 122 us -> 110 us (0.902)
  Pallas kernels: 116 us -> 110 us
  local copies, waits for them, and re-layouts: 5.46 us -> 0 us
    pallas_call x1, Pallas kernels: 116 us -> 107 us  [body(): pl.pallas_call(functools.partial(kernel, nz), out_shape=(jax.ShapeDtypeSt...]
    unnamed x4 -> x0, local copies, waits for them, and re-layouts: 2.85 us -> none
    pad x1 -> x0, local copies, waits for them, and re-layouts: 2.61 us -> none  [body(): jnp.pad(projections, ((0, 0), (0, PAD - HEAD), (0, 0)))]
    pallas_call x0 -> x1, Pallas kernels: none -> 2.47 us  [body(): pl.pallas_call(functools.partial(finish, 1.0 / (4 * nz)), out_shape=(jax....]
where the time goes in v2:
time: 110 us
  Pallas kernels  110 us (100%)
    pallas_call x1, Pallas kernels, body(): pl.pallas_call(functools.partial(kernel, nz), out_shape=(jax.ShapeDtypeSt...  107 us
    pallas_call x1, Pallas kernels, body(): pl.pallas_call(functools.partial(finish, 1.0 / (4 * nz)), out_shape=(jax....  2.47 us

profile of v2, /device:TPU:1, one launch (start us, length us, event | category | flops | bytes accessed | tf_op | source)
XLA Modules:
  0.0 110.3 jit_solution(1856461724498733357)
XLA Ops:
  0.6 107.2 %shard_map.59 = (bf16[16,128,128]{2,1,0:T(8,128)(2,1)}, bf16[2,2,2,8,16,256]{5,4,3,2,1,0:T(8,128)(2,1)}) custom-call(bf16[2,64,1920]{2,1,0:T(8,128)(2,1)} %bitcast.4, bf16[3,120,1920]{2,1,0:T(8,128)(2,1)} %w.1, bf16[128,1920]{1,0:T(8,128)(2,1)} %bitcast.5, s32[16,128]{1,0:T(8,128)} %bitcast.6), custom_call_target="tpu_custom_call" | custom-call | tf_op jit(solution)/shard_map/pallas_call | solution.py:456
  107.8 2.5 %shard_map.60 = (bf16[128,1920]{1,0:T(8,128)(2,1)}, f32[120,1920]{1,0:T(8,128)}) custom-call(bf16[16,128,128]{2,1,0:T(8,128)(2,1)} %get-tuple-element.6.cr_in, bf16[2,2,2,8,16,256]{5,4,3,2,1,0:T(8,128)(2,1)} %get-tuple-element.7.re_in), custom_call_target="tpu_custom_call" | custom-call | tf_op jit(solution)/shard_map/pallas_call | solution.py:504

commit v3 on v2

--- a/solution.py
+++ b/solution.py
@@ -24,10 +24,11 @@
 
 
 def kernel(
-    nz, feat, w, cot, seg, CR, RE,
-    G, WR, WA, CO, CT, DO, QKV, QS, SEGC, EB, INV, VRT, CX, AB, AS, PB, RA, PA, RB, PC, RC, PD,
-    ring_s, ring_r, loc, w_s, w_r, wz_s, wz_r, wc_s, wc_r, qs_s, qs_r, do_s, do_r, cx_s, cx_r,
-    vr_s, vr_r, a_s, a_r, b_s, b_r, c_s, c_r, d_s, d_r, e_s, e_r,
+    nz, feat, w, cot, seg, ctx_out, re_out,
+    G, WR, WA, CO, CT, XO, DO, QKV, QS, SEGC, EB, INV, VRT, CP, XC, CR, CF,
+    AB, AS, PB, RA, PA, RB, PC, RC, PD, RE,
+    ring_s, ring_r, loc, w_s, w_r, wz_s, wz_r, wc_s, wc_r, qs_s, qs_r, dx_s, dx_r, do_s, do_r,
+    xc_s, xc_r, cx_s, cx_r, vr_s, vr_r, a_s, a_r, b_s, b_r, c_s, c_r, d_s, d_r, e_s, e_r,
 ):
     ny = G.shape[0]
     ns = 2 * ny
@@ -130,10 +131,18 @@
         w_x(p).start()
 
     own_cot.wait()
-    for h in range(ns):
-        CT[h] = jnp.zeros((ROWS, PAD), BF16)
-        CT[h, :, 0:HEAD] = CO[:, h * HEAD : (h + 1) * HEAD]
-    DO[sq] = CT[sq]
+    for r in range(ny):
+        left = CO[:, 2 * r * HEAD : (2 * r + 1) * HEAD]
+        right = CO[:, (2 * r + 1) * HEAD : (2 * r + 2) * HEAD]
+        XO[r] = jnp.zeros((ROWS, PAD), BF16)
+        XO[r, :, 0:HEAD] = jnp.where(xlo == 0, right, left)
+        CT[r, xlo] = jnp.zeros((ROWS, PAD), BF16)
+        CT[r, xlo, :, 0:HEAD] = jnp.where(xlo == 0, left, right)
+
+    def dx_copy(col):
+        return remote(XO, CT.at[:, col], dx_s, dx_r, (dp, peer_x))
+
+    dx_copy(xlo).start()
 
     def label_col(b, carry):
         row = seg[pl.ds(b, 1), :].astype(F32)
@@ -167,15 +176,23 @@
             QS.at[shard], QKV.at[2 * shard + xlo], qs_s.at[shard], qs_r.at[shard], (dp, peer_x)
         )
 
-    def project(shard):
+    def project(shard, apart=False):
         x = G[shard].reshape(ROWS, width)
-        wall = WA[...].reshape(6 * PAD, width)
-        r = lax.dot_general(x, wall, NT, preferred_element_type=F32).astype(BF16)
+
+        def heads(wall):
+            wall = wall.reshape(-1, width)
+            return lax.dot_general(x, wall, NT, preferred_element_type=F32).astype(BF16)
+
+        if apart:
+            near, far = heads(WA[0]), heads(WA[1])
+        else:
+            both = heads(WA[...])
+            near, far = both[:, : 3 * PAD], both[:, 3 * PAD :]
         for p in range(3):
-            QS[shard, p] = r[:, (3 + p) * PAD : (4 + p) * PAD]
+            QS[shard, p] = far[:, p * PAD : (p + 1) * PAD]
         qs_copy(shard).start()
         for p in range(3):
-            QKV[2 * shard + xlo, p] = r[:, p * PAD : (p + 1) * PAD]
+            QKV[2 * shard + xlo, p] = near[:, p * PAD : (p + 1) * PAD]
 
     def qs_wait(shard):
         b = 2 * shard + (1 - xlo)
@@ -183,15 +200,8 @@
             QS.at[shard], QKV.at[b], qs_s.at[shard], qs_r.at[shard], (dp, peer_x)
         ).wait_recv()
 
-    def do_copy(to):
-        return remote(CT.at[to], DO.at[sq], do_s.at[to], do_r.at[sq], (dp, to))
-
-    def do_start(cross):
-        col = xlo + cross - 2 * cross * xlo
-        for d in (4, 3, -3, 2, -2, 1, -1):
-            do_copy(2 * at_y(d) + col).start()
-        if cross:
-            do_copy(2 * y + col).start()
+    def do_copy(r):
+        return remote(CT.at[r], DO.at[y], do_s.at[r], do_r.at[y], (dp, 2 * r + xlo))
 
     scale = HEAD ** (-0.5) * LOG2E
 
@@ -221,7 +231,14 @@
             ctx += lax.dot_general(e, rows_of(2, r), NN, preferred_element_type=F32)
         inv = jnp.broadcast_to(1.0 / jnp.sum(total, axis=1, keepdims=True), (2 * ROWS, PAD))
         INV[i] = inv
-        CX[pl.ds(2 * i, 2)] = (ctx * inv).astype(BF16).reshape(2, ROWS, PAD)
+        ctx = (ctx * inv).astype(BF16)
+        left, right = ctx[:ROWS], ctx[ROWS:]
+        XC[i] = jnp.where(xlo == 0, right, left)
+        xc_copy(i, xlo).start()
+        CP[i, xlo] = jnp.where(xlo == 0, left, right)
+
+    def xc_copy(i, head):
+        return remote(XC.at[i], CP.at[i, head], xc_s.at[i], xc_r.at[i], (dp, peer_x))
 
     def attend_at(d, carry):
         attend(at_y(d))
@@ -236,43 +253,46 @@
     project(at_y(1))
     project(at_y(-1))
     arrive(4)
-    do_start(0)
+    dx_copy(1 - xlo).wait_recv()
+    for d in (4, 3, -3):
+        do_copy(at_y(d)).start()
+    DO[y] = CT[y]
     project(at_y(2))
     project(at_y(-2))
     arrive(5)
+    for d in (2, -2, 1, -1):
+        do_copy(at_y(d)).start()
     project(at_y(3))
     project(at_y(-3))
     for d in (0, 1, -1, 2, -2):
         qs_wait(at_y(d))
     attend(y)
     arrive(6)
-    project(at_y(4))
-    do_start(1)
+    project(at_y(4), apart=True)
     qs_wait(at_y(3))
     qs_wait(at_y(-3))
+    lax.fori_loop(0, 2, lambda t, carry: attend_at(1 + 6 * t, carry), 0)
     qs_wait(at_y(4))
-    lax.fori_loop(1, ny, attend_at, 0)
+    lax.fori_loop(2, ny - 1, attend_at, 0)
 
     def vr_copy(r):
-        return remote(AS.at[r], AB.at[xlo, r], vr_s.at[r], vr_r.at[r], (dp, peer_x))
+        return remote(AS.at[r], AB.at[1, r], vr_s.at[r], vr_r.at[r], (dp, peer_x))
 
     def value_rows_out(r):
         v = VRT[r].astype(BF16)
         left, right = v[:, :PAD], v[:, PAD:]
         AS[r] = jnp.where(xlo == 0, right, left)
         vr_copy(r).start()
-        AB[xlo, r] = jnp.where(xlo == 0, left, right)
-
-    def do_wait(b):
-        @pl.when(b != sq)
-        def _():
-            remote(CT.at[b], DO.at[b], do_s.at[b], do_r.at[b], (dp, b)).wait_recv()
+        AB[0, r] = jnp.where(xlo == 0, left, right)
 
     def value_step(t, carry):
         i = lax.rem(y + 4 + t, ny)
-        do_wait(2 * i)
-        do_wait(2 * i + 1)
-        up = DO[pl.ds(2 * i, 2)].reshape(2 * ROWS, PAD).astype(F32) * INV[i]
+
+        @pl.when(i != y)
+        def _():
+            remote(CT.at[i], DO.at[i], do_s.at[i], do_r.at[i], (dp, 2 * i + xlo)).wait_recv()
+
+        up = DO[i].reshape(2 * ROWS, PAD).astype(F32) * INV[i]
         up = up.astype(BF16)
         for n in range(2 * REACH + 1):
             r = lax.rem(i + n - REACH + ny, ny)
@@ -288,50 +308,54 @@
     for d in range(2, 6):
         value_rows_out(at_y(d))
 
-    def cx_copy(b):
-        return remote(CX.at[b], CR.at[sq], cx_s.at[b], cx_r.at[sq], (dp, b))
-
-    def cx_start(d, carry):
-        cx_copy(lax.rem(sq + d, ns)).start()
-        return carry
-
-    lax.fori_loop(1, ns, cx_start, 0)
-    CR[sq] = CX[sq]
-
+    def cx_copy(r):
+        return remote(CP.at[r], CR.at[y], cx_s.at[r], cx_r.at[y], (dp, 2 * r + xlo))
+
+    for d in (4, 3, -3, 2, -2, 1, -1):
+        xc_copy(at_y(d), 1 - xlo).wait_recv()
+        cx_copy(at_y(d)).start()
+    xc_copy(y, 1 - xlo).wait_recv()
+    CR[y] = CP[y]
+
+    lanes = GROUP // STREAMS
+
+    def a_copy(u, h):
+        return remote(PB.at[u, other, h], RA.at[u, h], a_s.at[u, h], a_r.at[u, h], (peer_core, sq))
+
+    def product(h):
+        lhs = jnp.concatenate([AB[h, t] for t in range(ny)], axis=1)
+        for u in range(STREAMS):
+            for g in range(4):
+                lo = (4 * u + g) * lanes
+                hi = min(lo + lanes, width)
+                rhs = G[:, :, :, lo:hi].reshape(ny * ROWS, hi - lo)
+                part = lax.dot_general(lhs, rhs, NN, preferred_element_type=F32).astype(BF16)
+                if hi - lo < lanes:
+                    part = jnp.concatenate([part, jnp.zeros((PAD, lanes - hi + lo), BF16)], axis=1)
+                PB[u, g % 2, h, g // 2] = part.reshape(8, 16, lanes)
+            a_copy(u, h).start()
+
+    def b_copy(u, n):
+        h, g = (1, xhi) if n == 0 else (0, 1 - xhi) if n == 1 else (1, 1 - xhi)
+        dev = (dp if n == 0 else peer_xhi, sq if n == 1 else peer_x)
+        return remote(PA.at[u, h, g], RB.at[u, n], b_s.at[u, n], b_r.at[u, n], dev)
+
+    def core_sum(u, h):
+        a_copy(u, h).wait_recv()
+        for g in range(2):
+            PA[u, h, g] = (PB[u, core, h, g].astype(F32) + RA[u, h, g].astype(F32)).astype(BF16)
+
+    product(0)
+    for u in range(STREAMS):
+        core_sum(u, 0)
+        b_copy(u, 1).start()
     for r in range(ny):
-        remote(AS.at[r], AB.at[1 - xlo, r], vr_s.at[r], vr_r.at[r], (dp, peer_x)).wait_recv()
-    lhs = jnp.concatenate(
-        [jnp.concatenate([AB[h, t] for t in range(ny)], axis=1) for h in range(2)], axis=0
-    )
-    lanes = GROUP // STREAMS
-
-    def a_copy(u):
-        return remote(PB.at[u, other], RA.at[u], a_s.at[u], a_r.at[u], (peer_core, sq))
-
-    for u in range(STREAMS):
-        for g in range(4):
-            lo = g * GROUP + u * lanes
-            hi = min(lo + lanes, width)
-            rhs = G[:, :, :, lo:hi].reshape(ny * ROWS, hi - lo)
-            part = lax.dot_general(lhs, rhs, NN, preferred_element_type=F32).astype(BF16)
-            if hi - lo < lanes:
-                part = jnp.concatenate([part, jnp.zeros((2 * PAD, lanes - hi + lo), BF16)], axis=1)
-            for h in range(2):
-                PB[u, g % 2, h, g // 2] = part[h * PAD : (h + 1) * PAD].reshape(8, 16, lanes)
-        a_copy(u).start()
-
-    def b_copy(u, n):
-        hi, lo = (xhi, 1 - xlo) if n == 0 else (1 - xhi, xlo) if n == 1 else (1 - xhi, 1 - xlo)
-        dev = (dp if n == 0 else peer_xhi, sq if n == 1 else peer_x)
-        return remote(PA.at[u, lo, hi], RB.at[u, n], b_s.at[u, n], b_r.at[u, n], dev)
-
-    for u in range(STREAMS):
-        a_copy(u).wait_recv()
-        for h in range(2):
-            for g in range(2):
-                PA[u, h, g] = (PB[u, core, h, g].astype(F32) + RA[u, h, g].astype(F32)).astype(BF16)
-        for n in (1, 2, 0):
-            b_copy(u, n).start()
+        vr_copy(r).wait_recv()
+    product(1)
+    for u in range(STREAMS):
+        core_sum(u, 1)
+        b_copy(u, 2).start()
+        b_copy(u, 0).start()
 
     rows = 8 // nz
 
@@ -341,13 +365,14 @@
             PC.at[u, pl.ds(to * rows, rows)], RC.at[u, d], c_s.at[u, d], c_r.at[u, d], (z_dev(d), sq)
         )
 
-    for u in range(STREAMS):
-        total = PA[u, xlo, xhi].astype(F32)
-        for n in range(3):
+    by_reach = sorted(range(1, nz), key=lambda d: -min(d, nz - d))
+    for u in range(STREAMS):
+        total = PA[u, 0, xhi].astype(F32)
+        for n in (1, 0, 2):
             b_copy(u, n).wait_recv()
             total += RB[u, n].astype(F32)
         PC[u] = total.astype(BF16)
-        for d in range(1, nz):
+        for d in by_reach:
             c_copy(u, d).start()
 
     def d_copy(u, d, frm):
@@ -365,7 +390,7 @@
             c_copy(u, d).wait_recv()
             total += RC[u, d].astype(F32)
         PD[u] = total.astype(BF16)
-        for d in range(1, nz):
+        for d in by_reach:
             d_copy(u, d, z).start()
         RE[u, xhi, core, pl.ds(z * rows, rows)] = total.astype(BF16)
 
@@ -376,26 +401,27 @@
         dev = (peer_xhi if n == 0 else peer_core, sq)
         return remote(ref, ref, e_s.at[u, n], e_r.at[u, n], dev)
 
+    for d in range(1, ny):
+        r = at_y(d)
+        remote(CP.at[r], CR.at[r], cx_s.at[r], cx_r.at[r], (dp, 2 * r + xlo)).wait_recv()
+    for h in range(ns):
+        CF[:, h * HEAD : (h + 1) * HEAD] = CR[h // 2, h % 2, :, 0:HEAD]
+    ctx_copy = pltpu.make_async_copy(CF, ctx_out, loc.at[0])
+    ctx_copy.start()
+
     for u in range(STREAMS):
         for d in range(1, nz):
             d_copy(u, d, lax.rem(z + nz - d, nz)).wait_recv()
         e_copy(u, 0).start()
         e_copy(u, 1).start()
-
-    def cx_wait(b, carry):
-        @pl.when(b != sq)
-        def _():
-            remote(CX.at[b], CR.at[b], cx_s.at[b], cx_r.at[b], (dp, b)).wait_recv()
-            cx_copy(b).wait_send()
-            do_copy(b).wait_send()
-
-        return carry
-
-    lax.fori_loop(0, ns, cx_wait, 0)
-
     for u in range(STREAMS):
         e_copy(u, 0, True).wait_recv()
         e_copy(u, 2).start()
+    re_copies = [pltpu.make_async_copy(RE.at[u], re_out.at[u], loc.at[1 + u]) for u in range(STREAMS)]
+    for u in range(STREAMS):
+        for n in range(1, 3):
+            e_copy(u, n, True).wait_recv()
+        re_copies[u].start()
 
     for k in range(last):
         for dirn in range(2):
@@ -405,38 +431,54 @@
         w_z(p, zlo).wait_send()
         w_c(p, core, zlo, 0).wait_send()
         w_c(p, core, 1 - zlo, 1).wait_send()
+    dx_copy(xlo).wait_send()
     for r in range(ny):
         qs_copy(r).wait_send()
+        xc_copy(r, xlo).wait_send()
         vr_copy(r).wait_send()
-    for u in range(STREAMS):
-        a_copy(u).wait_send()
+    for d in range(1, ny):
+        do_copy(at_y(d)).wait_send()
+        cx_copy(at_y(d)).wait_send()
+    for u in range(STREAMS):
+        for h in range(2):
+            a_copy(u, h).wait_send()
         for n in range(3):
             b_copy(u, n).wait_send()
+            e_copy(u, n).wait_send()
         for d in range(1, nz):
             c_copy(u, d).wait_send()
             d_copy(u, d, z).wait_send()
-        for n in range(1, 3):
-            e_copy(u, n, True).wait_recv()
-        for n in range(3):
-            e_copy(u, n).wait_send()
-
-
-def finish(scale, cr_in, re_in, ctx_out, grad_out, cr, re, sem):
-    copies = [pltpu.make_async_copy(*pair, sem.at[n]) for n, pair in enumerate(((cr_in, cr), (re_in, re)))]
-    for copy in copies:
-        copy.start()
-    copies[0].wait()
-    for h in range(cr.shape[0]):
-        ctx_out[:, h * HEAD : (h + 1) * HEAD] = cr[h, :, 0:HEAD]
-    copies[1].wait()
+    ctx_copy.wait()
+    for copy in re_copies:
+        copy.wait()
+
+
+def finish(scale, ctx_in, re_in, ctx_out, grad_out, ctx, re, grad, sem):
     lanes = GROUP // STREAMS
     width = grad_out.shape[1]
-    for u in range(STREAMS):
+    halves = [(4 * lanes * u, min(4 * lanes * (u + 1), width)) for u in range(STREAMS)]
+    parts = [pltpu.make_async_copy(re_in.at[u], re.at[u], sem.at[u]) for u in range(STREAMS)]
+    ctx_read = pltpu.make_async_copy(ctx_in, ctx, sem.at[STREAMS])
+    ctx_write = pltpu.make_async_copy(ctx, ctx_out, sem.at[STREAMS])
+    writes = [
+        pltpu.make_async_copy(grad.at[:, lo:hi], grad_out.at[:, lo:hi], sem.at[u])
+        for u, (lo, hi) in enumerate(halves)
+    ]
+    for copy in (*parts, ctx_read):
+        copy.start()
+    for u in range(STREAMS):
+        parts[u].wait()
         for g in range(4):
-            lo = g * GROUP + u * lanes
+            lo = (4 * u + g) * lanes
             hi = min(lo + lanes, width)
             block = re[u, g // 2, g % 2].reshape(PAD, lanes)[:HEAD, : hi - lo]
-            grad_out[:, lo:hi] = block.astype(F32) * scale
+            grad[:, lo:hi] = block.astype(F32) * scale
+        writes[u].start()
+        if u == 0:
+            ctx_read.wait()
+            ctx_write.start()
+    for copy in (*writes, ctx_write):
+        copy.wait()
 
 
 def body(nz, features, segment_ids, projections, cotangent):
@@ -452,29 +494,32 @@
     reach = 2 * REACH + 1
     held = pl.BlockSpec(memory_space=pltpu.VMEM)
     far = pl.BlockSpec(memory_space=pltpu.HBM)
-    kept = pl.BlockSpec(memory_space=pl.ANY)
-    cr, re = pl.pallas_call(
+    ctx, re = pl.pallas_call(
         functools.partial(kernel, nz),
         out_shape=(
-            jax.ShapeDtypeStruct((ns, ROWS, PAD), BF16),
+            jax.ShapeDtypeStruct((ROWS, width), BF16),
             jax.ShapeDtypeStruct((STREAMS, 2, 2, 8, 16, lanes), BF16),
         ),
         in_specs=[far, far, far, held],
-        out_specs=[held, held],
+        out_specs=[far, far],
         scratch_shapes=[
             vmem(ny, 2, HALF, width),
             vmem(3, HEAD, width),
             vmem(2, 3, 2, 2, HALF // 2, width),
             vmem(ROWS, width),
-            vmem(ns, ROWS, PAD),
-            vmem(ns, ROWS, PAD),
+            vmem(ny, 2, ROWS, PAD),
+            vmem(ny, ROWS, PAD),
+            vmem(ny, 2, ROWS, PAD),
             vmem(ns, 3, ROWS, PAD),
             vmem(ny, 3, ROWS, PAD),
             pltpu.VMEM((ns, ROWS, ROWS), F32),
             vmem(ny, reach, 2 * ROWS, 2 * ROWS),
             pltpu.VMEM((ny, 2 * ROWS, PAD), F32),
             pltpu.VMEM((ny, PAD, 2 * ROWS), F32),
-            vmem(ns, ROWS, PAD),
+            vmem(ny, 2, ROWS, PAD),
+            vmem(ny, ROWS, PAD),
+            vmem(ny, 2, ROWS, PAD),
+            vmem(ROWS, width),
             vmem(2, ny, PAD, ROWS),
             vmem(ny, PAD, ROWS),
             vmem(STREAMS, 2, 2, 2, 8, 16, lanes),
@@ -484,14 +529,17 @@
             vmem(STREAMS, 8, 16, lanes),
             vmem(STREAMS, nz, rows, 16, lanes),
             vmem(STREAMS, rows, 16, lanes),
+            vmem(STREAMS, 2, 2, 8, 16, lanes),
             dma(2, ny - 1), dma(2, ny - 1),
             dma(3),
             dma(3), dma(3), dma(3), dma(3), dma(2, 3), dma(2, 3),
             dma(ny), dma(ny),
-            dma(ns), dma(ns),
-            dma(ns), dma(ns),
+            dma(), dma(),
             dma(ny), dma(ny),
-            dma(STREAMS), dma(STREAMS),
+            dma(ny), dma(ny),
+            dma(ny), dma(ny),
+            dma(ny), dma(ny),
+            dma(STREAMS, 2), dma(STREAMS, 2),
             dma(STREAMS, 3), dma(STREAMS, 3),
             dma(STREAMS, nz), dma(STREAMS, nz),
             dma(STREAMS, nz), dma(STREAMS, nz),
@@ -507,14 +555,15 @@
             jax.ShapeDtypeStruct((ROWS, width), BF16),
             jax.ShapeDtypeStruct((HEAD, width), F32),
         ),
-        in_specs=[kept, kept],
-        out_specs=[held, held],
+        in_specs=[far, far],
+        out_specs=[far, far],
         scratch_shapes=[
-            vmem(ns, ROWS, PAD),
+            vmem(ROWS, width),
             vmem(STREAMS, 2, 2, 8, 16, lanes),
-            dma(2),
+            pltpu.VMEM((HEAD, width), F32),
+            dma(STREAMS + 1),
         ],
-    )(cr, re)
+    )(ctx, re)
     return (ctx[None], grad)
 
 

time: 110 us -> 103 us (0.936)
  Pallas kernels: 110 us -> 102 us
    pallas_call x1, Pallas kernels: 107 us -> 100 us  [body(): pl.pallas_call(functools.partial(kernel, nz), out_shape=(jax.ShapeDtypeSt...]
where the time goes in v3:
time: 103 us
  Pallas kernels  102 us (99%)
    pallas_call x1, Pallas kernels, body(): pl.pallas_call(functools.partial(kernel, nz), out_shape=(jax.ShapeDtypeSt...  100 us
    pallas_call x1, Pallas kernels, body(): pl.pallas_call(functools.partial(finish, 1.0 / (4 * nz)), out_shape=(jax....  2.14 us

profile of v3, /device:TPU:1, one launch (start us, length us, event | category | flops | bytes accessed | tf_op | source)
XLA Modules:
  0.0 103.1 jit_solution(17466383839625601529)
XLA Ops:
  0.6 100.3 %shard_map.59 = (bf16[128,1920]{1,0:T(8,128)(2,1)}, bf16[2,2,2,8,16,256]{5,4,3,2,1,0:T(8,128)(2,1)}) custom-call(bf16[2,64,1920]{2,1,0:T(8,128)(2,1)} %bitcast.4, bf16[3,120,1920]{2,1,0:T(8,128)(2,1)} %w.1, bf16[128,1920]{1,0:T(8,128)(2,1)} %bitcast.5, s32[16,128]{1,0:T(8,128)} %bitcast.6), custom_call_target="tpu_custom_call" | custom-call | tf_op jit(solution)/shard_map/pallas_call | solution.py:497
  100.9 2.1 %shard_map.60 = (bf16[128,1920]{1,0:T(8,128)(2,1)}, f32[120,1920]{1,0:T(8,128)}) custom-call(bf16[128,1920]{1,0:T(8,128)(2,1)} %get-tuple-element.6.ctx_in, bf16[2,2,2,8,16,256]{5,4,3,2,1,0:T(8,128)(2,1)} %get-tuple-element.7.re_in), custom_call_target="tpu_custom_call" | custom-call | tf_op jit(solution)/shard_map/pallas_call | solution.py:552

commit v4 on v3

v4 whole, which is shorter than its diff:
```python
import functools

import jax
import jax.numpy as jnp
from jax import lax
from jax.experimental import pallas as pl
from jax.experimental.pallas import tpu as pltpu
from jax.sharding import PartitionSpec as P

HEAD = 120
PAD = 128
ROWS = 128
HALF = 64
REACH = 2
STREAMS = 4
GROUP = 512
RING, WALL, DX, QSENT, DSENT, XSENT, VSENT, CSENT, ASENT, BSENT, ZSENT, TSENT, ESENT = range(13)
LOG2E = 1.4426950408889634
MESH = pl.DeviceIdType.MESH
NT = (((1,), (1,)), ((), ()))
NN = (((1,), (0,)), ((), ()))
TN = (((0,), (0,)), ((), ()))
F32 = jnp.float32
BF16 = jnp.bfloat16


def kernel(
    nz, feat, w, cot, seg_in, ctx_out, re_out,
    seg, G, WR, WA, CO, CT, XO, DO, QKV, QS, SEGC, EB, INV, VRT, CP, XC, CR, CF,
    AB, AS, PB, RA, PA, RB, PC, RC, PD, RE,
    sent, ring_r, loc, w_r, wz_r, wc_r, qs_r, dx_r, do_r, xc_r, cx_r, vr_r, a_r, b_r, c_r, d_r, e_r,
):
    ny = G.shape[0]
    ns = 2 * ny
    width = feat.shape[2]
    dp, sq = lax.axis_index("dp"), lax.axis_index("seq")
    core = lax.rem(dp, 2)
    xhi = lax.rem(lax.div(dp, 2), 2)
    z = lax.div(dp, 4)
    zlo = lax.rem(z, 2)
    y = lax.div(sq, 2)
    xlo = lax.rem(sq, 2)
    other = 1 - core
    peer_x = sq + 1 - 2 * xlo
    peer_core = dp + 1 - 2 * core
    peer_xhi = dp + 2 - 4 * xhi
    peer_z = dp + 4 - 8 * zlo

    def remote(src, dst, kind, rsem, dev):
        return pltpu.make_async_remote_copy(
            src_ref=src,
            dst_ref=dst,
            send_sem=sent.at[kind],
            recv_sem=rsem,
            device_id=dev,
            device_id_type=MESH,
        )

    def landed(ref, sem):
        pltpu.make_async_copy(ref, ref, sem).wait()

    own_feat = pltpu.make_async_copy(feat, G.at[y], loc.at[0])
    own_w = pltpu.make_async_copy(w, WR, loc.at[1])
    own_cot = pltpu.make_async_copy(cot, CO, loc.at[2])
    own_seg = pltpu.make_async_copy(seg_in, seg, loc.at[3])
    for copy in (own_feat, own_w, own_cot, own_seg):
        copy.start()

    barrier = pltpu.get_barrier_semaphore()

    def hello(dev):
        pl.semaphore_signal(barrier, inc=1, device_id=dev, device_id_type=MESH)

    def hello_seq(d, carry):
        hello((dp, lax.rem(sq + d, ns)))
        return carry

    lax.fori_loop(1, ns, hello_seq, 0)
    hello((peer_core, sq))
    hello((peer_xhi, sq))
    hello((peer_xhi, peer_x))

    def z_dev(d):
        return lax.rem(z + d, nz) * 4 + lax.rem(dp, 4)

    def hello_z(d, carry):
        hello((z_dev(d), sq))
        return carry

    lax.fori_loop(1, nz, hello_z, 0)

    own_feat.wait()
    pl.semaphore_wait(barrier, ns - 1 + 3 + nz - 1)

    last = ny - 1

    def ring(dirn, k, at):
        hops = k // 2
        if dirn == 0:
            shard, half, to = lax.rem(at + ny - hops, ny), k % 2, lax.rem(sq + 2, ns)
        else:
            shard, half, to = lax.rem(at + hops, ny), 1 - k % 2, lax.rem(sq + ns - 2, ns)
        ref = G.at[shard, half]
        return remote(ref, ref, RING, ring_r.at[dirn, k], (dp, to))

    def ring_send(dirn, k):
        return ring(dirn, k, y)

    def ring_recv(dirn, k):
        return ring(dirn, k, lax.rem(y + ny - 1, ny) if dirn == 0 else lax.rem(y + 1, ny))

    for k in range(2):
        for dirn in range(2):
            ring_send(dirn, k).start()

    own_w.wait()
    quarter = HALF // 2
    for p in range(3):
        for c in range(4):
            lo = c * quarter
            hi = min(lo + quarter, HEAD)
            WA[0, p, c // 2, c % 2, 0 : hi - lo] = WR[p, lo:hi]
            if hi - lo < quarter:
                WA[0, p, c // 2, c % 2, hi - lo :] = jnp.zeros((quarter - hi + lo, width), BF16)
    def w_x(p):
        return remote(
            WA.at[0, p, core, zlo], WA.at[1, p, core, zlo], WALL, w_r.at[p], (dp, peer_x)
        )

    def w_z(p, at):
        ref = WA.at[1, p, core, at]
        return remote(ref, ref, WALL, wz_r.at[p], (peer_z, sq))

    def w_c(p, at):
        ref = WA.at[1, p, core, at]
        return remote(ref, ref, WALL, wc_r, (peer_core, sq))

    for p in range(3):
        w_x(p).start()

    own_cot.wait()
    for r in range(ny):
        left = CO[:, 2 * r * HEAD : (2 * r + 1) * HEAD]
        right = CO[:, (2 * r + 1) * HEAD : (2 * r + 2) * HEAD]
        XO[r] = jnp.zeros((ROWS, PAD), BF16)
        XO[r, :, 0:HEAD] = jnp.where(xlo == 0, right, left)
        CT[r, xlo] = jnp.zeros((ROWS, PAD), BF16)
        CT[r, xlo, :, 0:HEAD] = jnp.where(xlo == 0, left, right)

    def dx_copy(col):
        return remote(XO, CT.at[:, col], DX, dx_r, (dp, peer_x))

    dx_copy(xlo).start()

    def label_col(b, carry):
        row = seg[pl.ds(b, 1), :].astype(F32)
        SEGC[b] = jnp.broadcast_to(row, (ROWS, ROWS)).T
        return carry

    own_seg.wait()
    lax.fori_loop(0, ns, label_col, 0)
    VRT[...] = jnp.zeros_like(VRT)

    def at_y(d):
        return lax.rem(y + d + ny, ny)

    def arrive(k):
        for dirn in range(2):
            ring_recv(dirn, k).wait_recv()
            if k + 2 <= last - 1:
                ring_send(dirn, k + 2).start()

    for p in range(3):
        w_x(p).wait_recv()
        w_z(p, zlo).start()
        w_c(p, zlo).start()
    arrive(0)
    for p in range(3):
        w_z(p, 1 - zlo).wait_recv()
        w_c(p, 1 - zlo).start()
    arrive(1)

    def qs_copy(d):
        shard = at_y(d)
        n = 0 if abs(d) < 3 else abs(d) - 2
        return remote(QS.at[shard], QKV.at[2 * shard + xlo], QSENT, qs_r.at[n], (dp, peer_x))

    def project(d, apart=False):
        shard = at_y(d)
        x = G[shard].reshape(ROWS, width)

        def heads(wall):
            wall = wall.reshape(-1, width)
            return lax.dot_general(x, wall, NT, preferred_element_type=F32).astype(BF16)

        if apart:
            near, far = heads(WA[0]), heads(WA[1])
        else:
            both = heads(WA[...])
            near, far = both[:, : 3 * PAD], both[:, 3 * PAD :]
        for p in range(3):
            QS[shard, p] = far[:, p * PAD : (p + 1) * PAD]
        qs_copy(d).start()
        for p in range(3):
            QKV[2 * shard + xlo, p] = near[:, p * PAD : (p + 1) * PAD]

    def do_copy(d):
        r = at_y(d)
        n = 0 if abs(d) == 1 else (ny - d) % ny - 1
        return remote(CT.at[r], DO.at[y], DSENT, do_r.at[n], (dp, 2 * r + xlo))

    scale = HEAD ** (-0.5) * LOG2E

    def rows_of(p, r):
        return QKV[pl.ds(2 * r, 2), p].reshape(2 * ROWS, PAD)

    def attend(i):
        q = rows_of(0, i)
        col = SEGC[pl.ds(2 * i, 2)].reshape(2 * ROWS, PAD)
        parts = []
        for o in range(-REACH, REACH + 1):
            r = lax.rem(i + o + ny, ny)
            s = lax.dot_general(q, rows_of(1, r), NT, preferred_element_type=F32)
            for c in range(2):
                row = seg[pl.ds(2 * r + c, 1), :].astype(F32)
                parts.append(jnp.where(col == row, s[:, c * PAD : (c + 1) * PAD], -1e30))
        top = functools.reduce(jnp.maximum, parts)
        top = jnp.max(top, axis=1, keepdims=True)
        total = jnp.zeros((2 * ROWS, PAD), F32)
        ctx = jnp.zeros((2 * ROWS, PAD), F32)
        for n in range(2 * REACH + 1):
            left, right = (jnp.exp2((part - top) * scale) for part in parts[2 * n : 2 * n + 2])
            total += left + right
            e = jnp.concatenate([left.astype(BF16), right.astype(BF16)], axis=1)
            EB[i, n] = e
            r = lax.rem(i + n - REACH + ny, ny)
            ctx += lax.dot_general(e, rows_of(2, r), NN, preferred_element_type=F32)
        inv = jnp.broadcast_to(1.0 / jnp.sum(total, axis=1, keepdims=True), (2 * ROWS, PAD))
        INV[i] = inv
        ctx = (ctx * inv).astype(BF16)
        left, right = ctx[:ROWS], ctx[ROWS:]
        XC[i] = jnp.where(xlo == 0, right, left)
        xc_copy(i, xlo).start()
        CP[i, xlo] = jnp.where(xlo == 0, left, right)

    def xc_copy(i, head):
        return remote(XC.at[i], CP.at[i, head], XSENT, xc_r, (dp, peer_x))

    def attend_at(d, carry):
        attend(at_y(d))
        return carry

    arrive(2)
    landed(WA.at[1, :, other], wc_r)
    project(0)
    arrive(3)
    project(1)
    project(-1)
    arrive(4)
    dx_copy(1 - xlo).wait_recv()
    for d in (1, -1, 4, 3):
        do_copy(d).start()
    DO[y] = CT[y]
    project(2)
    project(-2)
    arrive(5)
    for d in (-3, 2, -2):
        do_copy(d).start()
    project(3)
    project(-3)
    landed(QS.at[pl.ds(0, 5)], qs_r.at[0])
    attend(y)
    arrive(6)
    project(4, apart=True)
    landed(QS.at[pl.ds(0, 2)], qs_r.at[1])
    lax.fori_loop(0, 2, lambda t, carry: attend_at(1 + 6 * t, carry), 0)

    def vr_copy(r):
        return remote(AS.at[r], AB.at[1, r], VSENT, vr_r, (dp, peer_x))

    def value_rows_out(r):
        v = VRT[r].astype(BF16)
        left, right = v[:, :PAD], v[:, PAD:]
        AS[r] = jnp.where(xlo == 0, right, left)
        vr_copy(r).start()
        AB[0, r] = jnp.where(xlo == 0, left, right)

    def value_step(i):
        up = DO[i].reshape(2 * ROWS, PAD).astype(F32) * INV[i]
        up = up.astype(BF16)
        for n in range(2 * REACH + 1):
            r = lax.rem(i + n - REACH + ny, ny)
            VRT[r] += lax.dot_general(up, EB[i, n], TN, preferred_element_type=F32)

    def value_at(d, carry):
        value_step(at_y(d))
        return carry

    value_step(y)
    landed(DO.at[pl.ds(0, 2)], do_r.at[0])
    lax.fori_loop(0, 2, lambda t, carry: value_at(1 + 6 * t, carry), 0)
    landed(QS.at[0], qs_r.at[2])

    def far_rows(d, carry):
        attend(at_y(d))

        @pl.when(d > 2)
        def _():
            landed(DO.at[at_y(d - 1)], do_r.at[d - 2])
            value_step(at_y(d - 1))

        @pl.when(d > 3)
        def _():
            value_rows_out(at_y(d - 3))

        return carry

    lax.fori_loop(2, ny - 1, far_rows, 0)
    landed(DO.at[at_y(-2)], do_r.at[ny - 3])
    value_step(at_y(-2))
    for d in (4, 5, 6, 7, 0):
        value_rows_out(at_y(d))

    def cx_copy(r):
        return remote(CP.at[r], CR.at[y], CSENT, cx_r, (dp, 2 * r + xlo))

    lanes = GROUP // STREAMS

    def a_copy(u, h):
        return remote(PB.at[u, other, h], RA.at[u, h], ASENT, a_r.at[u, h], (peer_core, sq))

    def product(h):
        lhs = jnp.concatenate([AB[h, t] for t in range(ny)], axis=1)
        for u in range(STREAMS):
            lo = 4 * u * lanes
            hi = min(lo + 4 * lanes, width)
            rhs = G[:, :, :, lo:hi].reshape(ny * ROWS, hi - lo)
            part = lax.dot_general(lhs, rhs, NN, preferred_element_type=F32).astype(BF16)
            if hi - lo < 4 * lanes:
                part = jnp.concatenate([part, jnp.zeros((PAD, 4 * lanes - hi + lo), BF16)], axis=1)
            for g in range(4):
                block = part[:, g * lanes : (g + 1) * lanes]
                PB[u, g % 2, h, g // 2] = block.reshape(8, 16, lanes)
            a_copy(u, h).start()

    def b_copy(u, n):
        h, g = (1, xhi) if n == 0 else (0, 1 - xhi) if n == 1 else (1, 1 - xhi)
        dev = (dp if n == 0 else peer_xhi, sq if n == 1 else peer_x)
        return remote(PA.at[u, h, g], RB.at[u, n], BSENT, b_r.at[u], dev)

    def core_sum(u, h):
        a_copy(u, h).wait_recv()
        for g in range(2):
            PA[u, h, g] = (PB[u, core, h, g].astype(F32) + RA[u, h, g].astype(F32)).astype(BF16)

    product(0)
    for u in range(STREAMS):
        core_sum(u, 0)
        b_copy(u, 1).start()
    landed(AS, vr_r)
    product(1)
    landed(XC, xc_r)
    for d in (4, 3, -3, 2, -2, 1, -1):
        cx_copy(at_y(d)).start()
    CR[y] = CP[y]
    for u in range(STREAMS):
        core_sum(u, 1)
        b_copy(u, 2).start()
        b_copy(u, 0).start()

    rows = 8 // nz

    def c_copy(u, d):
        to = lax.rem(z + d, nz)
        return remote(
            PC.at[u, pl.ds(to * rows, rows)], RC.at[u, d], ZSENT, c_r.at[u], (z_dev(d), sq)
        )

    by_reach = sorted(range(1, nz), key=lambda d: -min(d, nz - d))
    for u in range(STREAMS):
        total = PA[u, 0, xhi].astype(F32)
        landed(RB.at[u], b_r.at[u])
        for n in range(3):
            total += RB[u, n].astype(F32)
        PC[u] = total.astype(BF16)
        for d in by_reach:
            c_copy(u, d).start()

    def d_copy(u, d):
        into = RE.at[u, xhi, core, pl.ds(z * rows, rows)]
        return remote(PD.at[u], into, TSENT, d_r.at[u], (z_dev(d), sq))

    for u in range(STREAMS):
        total = PC[u, pl.ds(z * rows, rows)].astype(F32)
        landed(RC.at[u, pl.ds(1, nz - 1)], c_r.at[u])
        for d in range(1, nz):
            total += RC[u, d].astype(F32)
        PD[u] = total.astype(BF16)
        for d in by_reach:
            d_copy(u, d).start()
        RE[u, xhi, core, pl.ds(z * rows, rows)] = total.astype(BF16)

    def e_copy(u, n, recv=False):
        c = other if recv and n > 0 else core
        hi = 1 - xhi if (n == 2) != (recv and n == 0) else xhi
        ref = RE.at[u, hi, c]
        dev = (peer_xhi if n == 0 else peer_core, sq)
        return remote(ref, ref, ESENT, e_r.at[u, min(n, 1)], dev)

    landed(CR.at[pl.ds(0, ny - 1)], cx_r)
    for h in range(ns):
        CF[:, h * HEAD : (h + 1) * HEAD] = CR[h // 2, h % 2, :, 0:HEAD]
    ctx_copy = pltpu.make_async_copy(CF, ctx_out, loc.at[0])
    ctx_copy.start()

    for u in range(STREAMS):
        landed(RC.at[u, pl.ds(1, nz - 1)], d_r.at[u])
        e_copy(u, 0).start()
        e_copy(u, 1).start()
    for u in range(STREAMS):
        e_copy(u, 0, True).wait_recv()
        e_copy(u, 2).start()
    re_copies = [pltpu.make_async_copy(RE.at[u], re_out.at[u], loc.at[1 + u]) for u in range(STREAMS)]
    for u in range(STREAMS):
        landed(RE.at[u, :, other], e_r.at[u, 1])
        re_copies[u].start()

    for kind, ref in (
        (RING, G.at[pl.ds(0, last)]),
        (WALL, WA.at[1]),
        (DX, XO),
        (QSENT, QS),
        (DSENT, CT.at[pl.ds(0, ny - 1)]),
        (XSENT, XC),
        (VSENT, AS),
        (CSENT, CP.at[pl.ds(0, ny - 1)]),
        (ASENT, RA),
        (BSENT, RB),
        (ZSENT, RC.at[:, pl.ds(1, nz - 1)]),
        (TSENT, RC.at[:, pl.ds(1, nz - 1)]),
        (ESENT, RB),
    ):
        landed(ref, sent.at[kind])
    ctx_copy.wait()
    for copy in re_copies:
        copy.wait()


def finish(scale, ctx_in, re_in, ctx_out, grad_out, ctx, re, grad, sem):
    lanes = GROUP // STREAMS
    width = grad_out.shape[1]
    halves = [(4 * lanes * u, min(4 * lanes * (u + 1), width)) for u in range(STREAMS)]
    parts = [pltpu.make_async_copy(re_in.at[u], re.at[u], sem.at[u]) for u in range(STREAMS)]
    ctx_read = pltpu.make_async_copy(ctx_in, ctx, sem.at[STREAMS])
    ctx_write = pltpu.make_async_copy(ctx, ctx_out, sem.at[STREAMS])
    writes = [
        pltpu.make_async_copy(grad.at[:, lo:hi], grad_out.at[:, lo:hi], sem.at[u])
        for u, (lo, hi) in enumerate(halves)
    ]
    for copy in (*parts, ctx_read):
        copy.start()
    for u in range(STREAMS):
        parts[u].wait()
        for g in range(4):
            lo = (4 * u + g) * lanes
            hi = min(lo + lanes, width)
            if lo >= hi:
                continue
            block = re[u, g // 2, g % 2].reshape(PAD, lanes)[:HEAD, : hi - lo]
            grad[:, lo:hi] = block.astype(F32) * scale
        writes[u].start()
        if u == 0:
            ctx_read.wait()
            ctx_write.start()
    for copy in (*writes, ctx_write):
        copy.wait()


def body(nz, features, segment_ids, projections, cotangent):
    ns = lax.axis_size("seq")
    ny = ns // 2
    width = features.shape[2]
    feat = features.reshape(2, HALF, width)
    seg = segment_ids.reshape(ns, ROWS)
    vmem = lambda *shape: pltpu.VMEM(shape, BF16)
    dma = lambda *shape: pltpu.SemaphoreType.DMA(shape)
    rows = 8 // nz
    lanes = GROUP // STREAMS
    reach = 2 * REACH + 1
    far = pl.BlockSpec(memory_space=pltpu.HBM)
    ctx, re = pl.pallas_call(
        functools.partial(kernel, nz),
        out_shape=(
            jax.ShapeDtypeStruct((ROWS, width), BF16),
            jax.ShapeDtypeStruct((STREAMS, 2, 2, 8, 16, lanes), BF16),
        ),
        in_specs=[far] * 4,
        out_specs=[far, far],
        scratch_shapes=[
            pltpu.VMEM((ns, ROWS), jnp.int32),
            vmem(ny, 2, HALF, width),
            vmem(3, HEAD, width),
            vmem(2, 3, 2, 2, HALF // 2, width),
            vmem(ROWS, width),
            vmem(ny, 2, ROWS, PAD),
            vmem(ny, ROWS, PAD),
            vmem(ny, 2, ROWS, PAD),
            vmem(ns, 3, ROWS, PAD),
            vmem(ny, 3, ROWS, PAD),
            pltpu.VMEM((ns, ROWS, ROWS), F32),
            vmem(ny, reach, 2 * ROWS, 2 * ROWS),
            pltpu.VMEM((ny, 2 * ROWS, PAD), F32),
            pltpu.VMEM((ny, PAD, 2 * ROWS), F32),
            vmem(ny, 2, ROWS, PAD),
            vmem(ny, ROWS, PAD),
            vmem(ny, 2, ROWS, PAD),
            vmem(ROWS, width),
            vmem(2, ny, PAD, ROWS),
            vmem(ny, PAD, ROWS),
            vmem(STREAMS, 2, 2, 2, 8, 16, lanes),
            vmem(STREAMS, 2, 2, 8, 16, lanes),
            vmem(STREAMS, 2, 2, 8, 16, lanes),
            vmem(STREAMS, 3, 8, 16, lanes),
            vmem(STREAMS, 8, 16, lanes),
            vmem(STREAMS, nz, rows, 16, lanes),
            vmem(STREAMS, rows, 16, lanes),
            vmem(STREAMS, 2, 2, 8, 16, lanes),
            dma(13),
            dma(2, ny - 1),
            dma(1 + max(3, STREAMS)),
            dma(3), dma(3), dma(),
            dma(3),
            dma(), dma(ny - 2),
            dma(), dma(), dma(),
            dma(STREAMS, 2),
            dma(STREAMS), dma(STREAMS), dma(STREAMS),
            dma(STREAMS, 2),
        ],
        compiler_params=pltpu.CompilerParams(
            collective_id=0, has_side_effects=True, vmem_limit_bytes=62 * 1024 * 1024
        ),
    )(feat, projections, cotangent[0], seg)
    ctx, grad = pl.pallas_call(
        functools.partial(finish, 1.0 / (4 * nz)),
        out_shape=(
            jax.ShapeDtypeStruct((ROWS, width), BF16),
            jax.ShapeDtypeStruct((HEAD, width), F32),
        ),
        in_specs=[far, far],
        out_specs=[far, far],
        scratch_shapes=[
            vmem(ROWS, width),
            vmem(STREAMS, 2, 2, 8, 16, lanes),
            pltpu.VMEM((HEAD, width), F32),
            dma(STREAMS + 1),
        ],
    )(ctx, re)
    return (ctx[None], grad)


def solution(mesh):
    in_specs = (P("dp", "seq", None), P("dp", None), P(None, "seq", None), P("dp", "seq", None))
    out_specs = (P("dp", "seq", None), P("seq", None))
    step = functools.partial(body, mesh.shape["dp"] // 4)
    return jax.shard_map(step, mesh=mesh, in_specs=in_specs, out_specs=out_specs, check_vma=False)
```

time: 103 us -> 101 us (0.981)
  Pallas kernels: 102 us -> 99.9 us
    pallas_call x1, Pallas kernels: 100 us -> 97.6 us  [body(): pl.pallas_call(functools.partial(kernel, nz), out_shape=(jax.ShapeDtypeSt...]
where the time goes in v4:
time: 101 us
  Pallas kernels  99.9 us (99%)
    pallas_call x1, Pallas kernels, body(): pl.pallas_call(functools.partial(kernel, nz), out_shape=(jax.ShapeDtypeSt...  97.6 us
    pallas_call x1, Pallas kernels, body(): pl.pallas_call(functools.partial(finish, 1.0 / (4 * nz)), out_shape=(jax....  2.33 us

profile of v4, /device:TPU:1, one launch (start us, length us, event | category | flops | bytes accessed | tf_op | source)
XLA Modules:
  0.0 100.5 jit_solution(3549761472081734524)
XLA Ops:
  0.6 97.6 %shard_map.59 = (bf16[128,1920]{1,0:T(8,128)(2,1)}, bf16[4,2,2,8,16,128]{5,4,3,2,1,0:T(8,128)(2,1)}) custom-call(bf16[2,64,1920]{2,1,0:T(8,128)(2,1)} %bitcast.4, bf16[3,120,1920]{2,1,0:T(8,128)(2,1)} %w.1, bf16[128,1920]{1,0:T(8,128)(2,1)} %bitcast.5, s32[16,128]{1,0:T(8,128)} %bitcast.6), custom_call_target="tpu_custom_call" | custom-call | tf_op jit(solution)/shard_map/pallas_call | solution.py:491
  98.2 2.3 %shard_map.60 = (bf16[128,1920]{1,0:T(8,128)(2,1)}, f32[120,1920]{1,0:T(8,128)}) custom-call(bf16[128,1920]{1,0:T(8,128)(2,1)} %get-tuple-element.6.ctx_in, bf16[4,2,2,8,16,128]{5,4,3,2,1,0:T(8,128)(2,1)} %get-tuple-element.7.re_in), custom_call_target="tpu_custom_call" | custom-call | tf_op jit(solution)/shard_map/pallas_call | solution.py:543

commit v5 on v4

--- a/solution.py
+++ b/solution.py
@@ -12,7 +12,7 @@
 ROWS = 128
 HALF = 64
 REACH = 2
-STREAMS = 4
+STREAMS = 2
 GROUP = 512
 RING, WALL, DX, QSENT, DSENT, XSENT, VSENT, CSENT, ASENT, BSENT, ZSENT, TSENT, ESENT = range(13)
 LOG2E = 1.4426950408889634
@@ -28,7 +28,7 @@
     nz, feat, w, cot, seg_in, ctx_out, re_out,
     seg, G, WR, WA, CO, CT, XO, DO, QKV, QS, SEGC, EB, INV, VRT, CP, XC, CR, CF,
     AB, AS, PB, RA, PA, RB, PC, RC, PD, RE,
-    sent, ring_r, loc, w_r, wz_r, wc_r, qs_r, dx_r, do_r, xc_r, cx_r, vr_r, a_r, b_r, c_r, d_r, e_r,
+    near, sent, ring_r, loc, w_r, wz_r, wc_r, qs_r, dx_r, do_r, xc_r, cx_r, vr_r, a_r, b_r, c_r, d_r, e_r,
 ):
     ny = G.shape[0]
     ns = 2 * ny
@@ -68,29 +68,31 @@
 
     barrier = pltpu.get_barrier_semaphore()
 
-    def hello(dev):
-        pl.semaphore_signal(barrier, inc=1, device_id=dev, device_id_type=MESH)
-
-    def hello_seq(d, carry):
-        hello((dp, lax.rem(sq + d, ns)))
-        return carry
-
-    lax.fori_loop(1, ns, hello_seq, 0)
-    hello((peer_core, sq))
-    hello((peer_xhi, sq))
-    hello((peer_xhi, peer_x))
-
     def z_dev(d):
-        return lax.rem(z + d, nz) * 4 + lax.rem(dp, 4)
-
-    def hello_z(d, carry):
-        hello((z_dev(d), sq))
-        return carry
-
-    lax.fori_loop(1, nz, hello_z, 0)
-
-    own_feat.wait()
-    pl.semaphore_wait(barrier, ns - 1 + 3 + nz - 1)
+        return lax.rem(z + d + nz, nz) * 4 + lax.rem(dp, 4)
+
+    y_near = [(dp, lax.rem(sq + d, ns)) for d in (2, ns - 2)]
+    x_near = [(dp, peer_x), (peer_xhi, peer_x)]
+    z_near = [(z_dev(d), sq) for d in (1, -1)]
+
+    def hello(sem, devs):
+        for dev in devs:
+            pl.semaphore_signal(sem, inc=1, device_id=dev, device_id_type=MESH)
+
+    hello(barrier, y_near + x_near + z_near + [(peer_core, sq)])
+    pl.semaphore_wait(barrier, 7)
+
+    def pass_on(step):
+        if step:
+            pl.semaphore_wait(near.at[step - 1], 2)
+            pl.semaphore_wait(near.at[step + 2], 2)
+        if step == 1:
+            pl.semaphore_wait(near.at[6], 2)
+        if step < 3:
+            hello(near.at[step], y_near)
+            hello(near.at[step + 3], z_near)
+        if step == 0:
+            hello(near.at[6], x_near)
 
     last = ny - 1
 
@@ -101,7 +103,8 @@
         else:
             shard, half, to = lax.rem(at + hops, ny), 1 - k % 2, lax.rem(sq + ns - 2, ns)
         ref = G.at[shard, half]
-        return remote(ref, ref, RING, ring_r.at[dirn, k], (dp, to))
+        src = feat.at[half] if k < 2 else ref
+        return remote(src, ref, RING, ring_r.at[dirn, k], (dp, to))
 
     def ring_send(dirn, k):
         return ring(dirn, k, y)
@@ -112,6 +115,7 @@
     for k in range(2):
         for dirn in range(2):
             ring_send(dirn, k).start()
+    pass_on(0)
 
     own_w.wait()
     quarter = HALF // 2
@@ -170,15 +174,17 @@
             if k + 2 <= last - 1:
                 ring_send(dirn, k + 2).start()
 
+    arrive(0)
+    pass_on(1)
     for p in range(3):
         w_x(p).wait_recv()
         w_z(p, zlo).start()
         w_c(p, zlo).start()
-    arrive(0)
     for p in range(3):
         w_z(p, 1 - zlo).wait_recv()
         w_c(p, 1 - zlo).start()
     arrive(1)
+    pass_on(2)
 
     def qs_copy(d):
         shard = at_y(d)
@@ -251,6 +257,8 @@
         return carry
 
     arrive(2)
+    pass_on(3)
+    own_feat.wait()
     landed(WA.at[1, :, other], wc_r)
     project(0)
     arrive(3)
@@ -258,13 +266,13 @@
     project(-1)
     arrive(4)
     dx_copy(1 - xlo).wait_recv()
-    for d in (1, -1, 4, 3):
+    for d in (1, -1, -2, -3):
         do_copy(d).start()
     DO[y] = CT[y]
     project(2)
     project(-2)
     arrive(5)
-    for d in (-3, 2, -2):
+    for d in (4, 3, 2):
         do_copy(d).start()
     project(3)
     project(-3)
@@ -525,6 +533,7 @@
             vmem(STREAMS, nz, rows, 16, lanes),
             vmem(STREAMS, rows, 16, lanes),
             vmem(STREAMS, 2, 2, 8, 16, lanes),
+            pltpu.SemaphoreType.REGULAR((7,)),
             dma(13),
             dma(2, ny - 1),
             dma(1 + max(3, STREAMS)),

time: 101 us -> 97.9 us (0.969)
  Pallas kernels: 99.9 us -> 97.2 us
    pallas_call x1, Pallas kernels: 97.6 us -> 95 us  [body(): pl.pallas_call(functools.partial(kernel, nz), out_shape=(jax.ShapeDtypeSt...]
where the time goes in v5:
time: 97.9 us; the launch traced here: 97.8 us
  Pallas kernels  97.2 us (99%)
    pallas_call x1, Pallas kernels, body(): pl.pallas_call(functools.partial(kernel, nz), out_shape=(jax.ShapeDtypeSt...  95 us
    pallas_call x1, Pallas kernels, body(): pl.pallas_call(functools.partial(finish, 1.0 / (4 * nz)), out_shape=(jax....  2.14 us

profile of v5, /device:TPU:1, one launch (start us, length us, event | category | flops | bytes accessed | tf_op | source)
XLA Modules:
  0.0 97.8 jit_solution(13091669666500433509)
XLA Ops:
  0.6 95.0 %shard_map.59 = (bf16[128,1920]{1,0:T(8,128)(2,1)}, bf16[2,2,2,8,16,256]{5,4,3,2,1,0:T(8,128)(2,1)}) custom-call(bf16[2,64,1920]{2,1,0:T(8,128)(2,1)} %bitcast.4, bf16[3,120,1920]{2,1,0:T(8,128)(2,1)} %w.1, bf16[128,1920]{1,0:T(8,128)(2,1)} %bitcast.5, s32[16,128]{1,0:T(8,128)} %bitcast.6), custom_call_target="tpu_custom_call" | custom-call | tf_op jit(solution)/shard_map/pallas_call | solution.py:499
  95.7 2.1 %shard_map.60 = (bf16[128,1920]{1,0:T(8,128)(2,1)}, f32[120,1920]{1,0:T(8,128)}) custom-call(bf16[128,1920]{1,0:T(8,128)(2,1)} %get-tuple-element.6.ctx_in, bf16[2,2,2,8,16,256]{5,4,3,2,1,0:T(8,128)(2,1)} %get-tuple-element.7.re_in), custom_call_target="tpu_custom_call" | custom-call | tf_op jit(solution)/shard_map/pallas_call | solution.py:552

commit v6 on v5

--- a/solution.py
+++ b/solution.py
@@ -12,7 +12,7 @@
 ROWS = 128
 HALF = 64
 REACH = 2
-STREAMS = 2
+STREAMS = 4
 GROUP = 512
 RING, WALL, DX, QSENT, DSENT, XSENT, VSENT, CSENT, ASENT, BSENT, ZSENT, TSENT, ESENT = range(13)
 LOG2E = 1.4426950408889634
@@ -180,11 +180,11 @@
         w_x(p).wait_recv()
         w_z(p, zlo).start()
         w_c(p, zlo).start()
+    arrive(1)
+    pass_on(2)
     for p in range(3):
         w_z(p, 1 - zlo).wait_recv()
         w_c(p, 1 - zlo).start()
-    arrive(1)
-    pass_on(2)
 
     def qs_copy(d):
         shard = at_y(d)
@@ -199,16 +199,21 @@
             wall = wall.reshape(-1, width)
             return lax.dot_general(x, wall, NT, preferred_element_type=F32).astype(BF16)
 
-        if apart:
-            near, far = heads(WA[0]), heads(WA[1])
-        else:
-            both = heads(WA[...])
-            near, far = both[:, : 3 * PAD], both[:, 3 * PAD :]
+        lane = lax.broadcasted_iota(jnp.int32, (ROWS, PAD), 1)
+        one = jnp.where(lane == HEAD, 1.0, 0.0).astype(BF16)
+
+        def block(cols, p):
+            part = cols[:, p * PAD : (p + 1) * PAD]
+            return part + one if p == 2 else part
+
+        both = None if apart else heads(WA[...])
+        far = heads(WA[1]) if apart else both[:, 3 * PAD :]
         for p in range(3):
-            QS[shard, p] = far[:, p * PAD : (p + 1) * PAD]
+            QS[shard, p] = block(far, p)
         qs_copy(d).start()
+        near = heads(WA[0]) if apart else both[:, : 3 * PAD]
         for p in range(3):
-            QKV[2 * shard + xlo, p] = near[:, p * PAD : (p + 1) * PAD]
+            QKV[2 * shard + xlo, p] = block(near, p)
 
     def do_copy(d):
         r = at_y(d)
@@ -232,16 +237,14 @@
                 parts.append(jnp.where(col == row, s[:, c * PAD : (c + 1) * PAD], -1e30))
         top = functools.reduce(jnp.maximum, parts)
         top = jnp.max(top, axis=1, keepdims=True)
-        total = jnp.zeros((2 * ROWS, PAD), F32)
         ctx = jnp.zeros((2 * ROWS, PAD), F32)
         for n in range(2 * REACH + 1):
             left, right = (jnp.exp2((part - top) * scale) for part in parts[2 * n : 2 * n + 2])
-            total += left + right
             e = jnp.concatenate([left.astype(BF16), right.astype(BF16)], axis=1)
             EB[i, n] = e
             r = lax.rem(i + n - REACH + ny, ny)
             ctx += lax.dot_general(e, rows_of(2, r), NN, preferred_element_type=F32)
-        inv = jnp.broadcast_to(1.0 / jnp.sum(total, axis=1, keepdims=True), (2 * ROWS, PAD))
+        inv = jnp.broadcast_to(1.0 / ctx[:, HEAD : HEAD + 1], (2 * ROWS, PAD))
         INV[i] = inv
         ctx = (ctx * inv).astype(BF16)
         left, right = ctx[:ROWS], ctx[ROWS:]
@@ -394,9 +397,12 @@
         for d in by_reach:
             c_copy(u, d).start()
 
+    def reach_of(d):
+        return 0 if min(d, nz - d) < 3 else 1
+
     def d_copy(u, d):
         into = RE.at[u, xhi, core, pl.ds(z * rows, rows)]
-        return remote(PD.at[u], into, TSENT, d_r.at[u], (z_dev(d), sq))
+        return remote(PD.at[u], into, TSENT, d_r.at[u, reach_of(d)], (z_dev(d), sq))
 
     for u in range(STREAMS):
         total = PC[u, pl.ds(z * rows, rows)].astype(F32)
@@ -408,12 +414,13 @@
             d_copy(u, d).start()
         RE[u, xhi, core, pl.ds(z * rows, rows)] = total.astype(BF16)
 
-    def e_copy(u, n, recv=False):
-        c = other if recv and n > 0 else core
-        hi = 1 - xhi if (n == 2) != (recv and n == 0) else xhi
-        ref = RE.at[u, hi, c]
-        dev = (peer_xhi if n == 0 else peer_core, sq)
-        return remote(ref, ref, ESENT, e_r.at[u, min(n, 1)], dev)
+    def e_copy(u, n):
+        ref = RE.at[u, xhi if n == 1 else 1 - xhi, core]
+        return remote(ref, ref, ESENT, e_r.at[u, 1], (peer_core, sq))
+
+    def e_piece(u, d):
+        ref = RE.at[u, xhi, core, pl.ds(lax.rem(z + d, nz) * rows, rows)]
+        return remote(ref, ref, ESENT, e_r.at[u, 0], (peer_xhi, sq))
 
     landed(CR.at[pl.ds(0, ny - 1)], cx_r)
     for h in range(ns):
@@ -421,12 +428,18 @@
     ctx_copy = pltpu.make_async_copy(CF, ctx_out, loc.at[0])
     ctx_copy.start()
 
-    for u in range(STREAMS):
-        landed(RC.at[u, pl.ds(1, nz - 1)], d_r.at[u])
-        e_copy(u, 0).start()
-        e_copy(u, 1).start()
-    for u in range(STREAMS):
-        e_copy(u, 0, True).wait_recv()
+    for part in range(2):
+        steps = [d for d in range(1, nz) if reach_of(d) == part]
+        for u in range(STREAMS):
+            if part == 0:
+                e_piece(u, 0).start()
+            landed(RC.at[u, pl.ds(1, len(steps))], d_r.at[u, part])
+            for d in steps:
+                e_piece(u, d).start()
+            if part == 1:
+                e_copy(u, 1).start()
+    for u in range(STREAMS):
+        landed(RE.at[u, 1 - xhi, core], e_r.at[u, 0])
         e_copy(u, 2).start()
     re_copies = [pltpu.make_async_copy(RE.at[u], re_out.at[u], loc.at[1 + u]) for u in range(STREAMS)]
     for u in range(STREAMS):
@@ -542,7 +555,7 @@
             dma(), dma(ny - 2),
             dma(), dma(), dma(),
             dma(STREAMS, 2),
-            dma(STREAMS), dma(STREAMS), dma(STREAMS),
+            dma(STREAMS), dma(STREAMS), dma(STREAMS, 2),
             dma(STREAMS, 2),
         ],
         compiler_params=pltpu.CompilerParams(

time: 97.9 us -> 96.9 us (0.990)
  Pallas kernels: 97.2 us -> 95.6 us
    pallas_call x1, Pallas kernels: 95 us -> 93.3 us  [body(): pl.pallas_call(functools.partial(kernel, nz), out_shape=(jax.ShapeDtypeSt...]
where the time goes in v6:
time: 96.9 us; the launch traced here: 96.2 us
  Pallas kernels  95.6 us (99%)
    pallas_call x1, Pallas kernels, body(): pl.pallas_call(functools.partial(kernel, nz), out_shape=(jax.ShapeDtypeSt...  93.3 us
    pallas_call x1, Pallas kernels, body(): pl.pallas_call(functools.partial(finish, 1.0 / (4 * nz)), out_shape=(jax....  2.33 us

profile of v6, /device:TPU:1, one launch (start us, length us, event | category | flops | bytes accessed | tf_op | source)
XLA Modules:
  0.0 96.2 jit_solution(10994715839083038764)
XLA Ops:
  0.6 93.3 %shard_map.59 = (bf16[128,1920]{1,0:T(8,128)(2,1)}, bf16[4,2,2,8,16,128]{5,4,3,2,1,0:T(8,128)(2,1)}) custom-call(bf16[2,64,1920]{2,1,0:T(8,128)(2,1)} %bitcast.4, bf16[3,120,1920]{2,1,0:T(8,128)(2,1)} %w.1, bf16[128,1920]{1,0:T(8,128)(2,1)} %bitcast.5, s32[16,128]{1,0:T(8,128)} %bitcast.6), custom_call_target="tpu_custom_call" | custom-call | tf_op jit(solution)/shard_map/pallas_call | solution.py:512
  93.9 2.3 %shard_map.60 = (bf16[128,1920]{1,0:T(8,128)(2,1)}, f32[120,1920]{1,0:T(8,128)}) custom-call(bf16[128,1920]{1,0:T(8,128)(2,1)} %get-tuple-element.6.ctx_in, bf16[4,2,2,8,16,128]{5,4,3,2,1,0:T(8,128)(2,1)} %get-tuple-element.7.re_in), custom_call_target="tpu_custom_call" | custom-call | tf_op jit(solution)/shard_map/pallas_call | solution.py:565
